TPU v7x, 128 devices: a whole 4x4x4 slice. The times are simulated.
128 devices in a mesh: space: 8 (over x, core), win: 16 (over z, y).
Axes of the slice: x: 4, y: 4, z: 4, core: 2. Of those that a mesh axis runs over, the one named last changes fastest.
Arguments:
- snapshots: bfloat16 [128, 24576, 256], P('win', 'space'), as said below
- modes: bfloat16 [128, 24576, 256], P('win', 'space'), may hold values from -0.5 to 0.5
- amp_re: float32 [128, 128], P('win'), may hold values from -5 to 5
- amp_im: float32 [128, 128], P('win'), may hold values from -5 to 5
- growth: float32 [128, 128], P('win'), may hold values from -0.01171875 to 0.001953125
- freq: float32 [128, 128], P('win'), may hold values from -3.140625 to 3.140625
- mode_count: int32 [128], P('win'), may hold values from 8 to 128
- slot_window: int32 [128], P('win'), may hold values from 0 to 127, as said below
Outputs:
- gram: float32 [128, 256, 256], P('win')
Inputs may be any that keep to these rules, and one draw needn't show every extreme that they name: slot_window is a permutation of the 128 windows; slot j holds a window of the same position in its block, slot_window[j] % 8 == j % 8; the 8 slots of one block hold windows of 8 different blocks. Each point's snapshots share one scale.
All inputs are finite; a program needn't handle non-finite values.
Results may differ from a plain program's by a relative error of at most 0.0026.
Values may be sent and summed in bfloat16 or wider, within the bound.
A program may use at most 192 MiB of HBM per device.

v0:
```python
import jax
import jax.numpy as jnp
from jax import lax
from jax.sharding import PartitionSpec as P

K = 128
S = 256
WIN_DEV = 8


def coefficients(amp_re, amp_im, growth, freq, mode_count):
    steps = jnp.arange(S).astype(jnp.float32)
    live = (jnp.arange(K, dtype=jnp.int32)[None, :] < mode_count[:, None]).astype(jnp.float32)
    decay = jnp.exp(growth[:, :, None] * steps) * live[:, :, None]
    angle = freq[:, :, None] * steps
    cosine = jnp.cos(angle)
    sine = jnp.sin(angle)
    real_part = (amp_re[:, :, None] * cosine - amp_im[:, :, None] * sine) * decay
    imag_part = (amp_re[:, :, None] * sine + amp_im[:, :, None] * cosine) * decay
    stacked = jnp.stack([real_part, -imag_part], axis=2)
    return stacked.reshape(amp_re.shape[0], 2 * K, S).astype(jnp.bfloat16)


def batch_grams(slabs, vectors, coef):
    recon = jnp.einsum("wpk,wks->wps", vectors, coef, preferred_element_type=jnp.float32)
    resid = (slabs.astype(jnp.float32) - recon).astype(jnp.bfloat16)
    return jnp.einsum("wps,wpt->wst", resid, resid, preferred_element_type=jnp.float32)


def on_device(snapshots, modes, amp_re, amp_im, growth, freq, mode_count, slot_window):
    nblocks = lax.axis_size("win")
    points_all = snapshots.shape[1] * lax.axis_size("space")
    coef = coefficients(amp_re, amp_im, growth, freq, mode_count)
    dest = slot_window // WIN_DEV
    place = slot_window % WIN_DEV
    vec_buf = jnp.zeros((nblocks,) + modes.shape[1:], jnp.bfloat16).at[dest].set(modes)
    coef_buf = jnp.zeros((nblocks, 2 * K, S), jnp.bfloat16).at[dest].set(coef)
    mark_buf = (
        jnp.zeros((nblocks, 128), jnp.bfloat16)
        .at[dest, place]
        .set(jnp.ones((WIN_DEV,), jnp.bfloat16))
    )
    got_vec, got_coef, got_mark = (
        lax.all_to_all(vec_buf, "win", split_axis=0, concat_axis=0, tiled=True),
        lax.all_to_all(coef_buf, "win", split_axis=0, concat_axis=0, tiled=True),
        lax.all_to_all(mark_buf, "win", split_axis=0, concat_axis=0, tiled=True),
    )
    marks = got_mark[:, :WIN_DEV].astype(jnp.int32)
    source = jnp.sum(jnp.arange(nblocks, dtype=jnp.int32)[:, None] * marks, axis=0)
    partial_value = batch_grams(snapshots, got_vec[source], got_coef[source])
    total = lax.psum(partial_value, "space")
    return total / points_all


def solution(mesh):
    return jax.shard_map(
        on_device,
        mesh=mesh,
        in_specs=(
            P("win", "space", None),
            P("win", "space", None),
            P("win", None),
            P("win", None),
            P("win", None),
            P("win", None),
            P("win"),
            P("win"),
        ),
        out_specs=P("win", None, None),
        check_vma=False,
    )
```

profile of v0, /device:TPU:0, one launch (start us, length us, event | category | flops | bytes accessed | tf_op | source)
XLA Modules:
  0.0 555.5 jit_solution(11417734754348130964)
XLA Ops:
  6.5 0.7 fusion.18
  7.2 0.9 scatter_fusion.1
  8.1 0.6 copy.20
  8.7 8.2 %all-to-all-start.1 = ((bf16[16,1,128]{2,1,0:T(2,128)(2,1)}), bf16[16,1,128]{2,1,0:T(2,128)(2,1)S(1)}, u32[]{:S(2)}, u32[]{:S(2)}) async-start(bf16[16,1,128]{2,1,0:T(2,128)(2,1)} %copy.20), calls=%async_computation.1 | async-start | bytes 16384 | tf_op jit(solution)/shard_map/all_to_all | solution.py:46
  16.9 0.7 fusion.14
  17.6 5.3 fusion.9
  22.9 0.1 pad_maximum_fusion
  23.1 0.6 copy.21
  23.6 0.2 copy.22
  23.9 1.5 broadcast_in_dim.14
  25.4 2.8 scatter_fusion.2
  28.2 0.0 all-to-all-done.1
  28.2 7.2 %all-to-all-start.2 = ((bf16[16,256,256]{2,1,0:T(8,128)(2,1)}), bf16[16,256,256]{2,1,0:T(8,128)(2,1)S(1)}, u32[]{:S(2)}, u32[]{:S(2)}) async-start(bf16[16,256,256]{2,1,0:T(8,128)(2,1)} %scatter_fusion.2), calls=%async_computation.2 | async-start | bytes 4194304 | tf_op jit(solution)/shard_map/all_to_all | solution.py:45
  35.5 8.3 %broadcast_in_dim.10 = bf16[16,3072,256]{2,1,0:T(8,128)(2,1)} broadcast(bf16[]{:T(256)} %constant.32.clone.1), dimensions={} | broadcast | bytes 25165826 | tf_op jit(solution)/shard_map/broadcast_in_dim | solution.py:36
  43.8 25.7 %scatter_fusion = bf16[16,3072,256]{2,1,0:T(8,128)(2,1)} fusion(bf16[16,3072,256]{2,1,0:T(8,128)(2,1)} %broadcast_in_dim.10, s32[8]{0:T(128)S(1)} %get-tuple-element.6, bf16[8,3072,256]{2,1,0:T(8,128)(2,1)} %param.9), kind=kCustom, calls=%fused_computation.2 | custom fusion | bytes 37748768 | tf_op jit(solution)/shard_map/scatter | solution.py:36
  69.5 0.0 all-to-all-done.2
  69.5 7.2 %all-to-all-start = ((bf16[16,3072,256]{2,1,0:T(8,128)(2,1)}), bf16[16,3072,256]{2,1,0:T(8,128)(2,1)}, u32[]{:S(2)}, u32[]{:S(2)}) async-start(bf16[16,3072,256]{2,1,0:T(8,128)(2,1)} %scatter_fusion), calls=%async_computation | async-start | bytes 50331648 | tf_op jit(solution)/shard_map/all_to_all | solution.py:44
  76.7 0.0 all-reduce.2.cloned.1.call-start
  76.8 0.6 gather_fusion.1
  77.4 369.2 %all-to-all-done = bf16[16,3072,256]{2,1,0:T(8,128)(2,1)} async-done(((bf16[16,3072,256]{2,1,0:T(8,128)(2,1)}), bf16[16,3072,256]{2,1,0:T(8,128)(2,1)}, u32[]{:S(2)}, u32[]{:S(2)}) %all-to-all-start) | async-done | bytes 25165856 | tf_op jit(solution)/shard_map/all_to_all | solution.py:44
  446.6 14.6 %gather_fusion = bf16[8,3072,256]{2,1,0:T(8,128)(2,1)} fusion(bf16[16,3072,256]{2,1,0:T(8,128)(2,1)} %all-to-all-done, s32[1024]{0:T(1024)S(1)} %pad_clamp_fusion), kind=kCustom, calls=%fused_computation | custom fusion | bytes 25165856 | tf_op jit(solution)/shard_map/gather | solution.py:50
  461.2 19.9 %fusion = f32[8,256,256]{2,1,0:T(8,128)} fusion(bf16[8,3072,256]{2,1,0:T(8,128)(2,1)} %param.8, bf16[8,3072,256]{2,1,0:T(8,128)(2,1)} %gather_fusion, bf16[8,256,256]{2,1,0:T(8,128)(2,1)S(1)} %gather_fusion.1), kind=kOutput, calls=%fused_computation.6 | convolution fusion | flops 6461325312 | bytes 28311552 | tf_op jit(solution)/shard_map/wps,wpt->wst/dot_general | solution.py:27
  481.2 0.0 all-reduce.2.cloned.1.call-update
  481.2 64.4 %all-reduce.2.cloned.1.call-done = f32[8,256,256]{2,1,0:T(8,128)} async-done(((f32[8,256,256]{2,1,0:T(8,128)}), f32[8,256,256]{2,1,0:T(8,128)}) %all-reduce.2.cloned.1.call-update) | async-done | bytes 2097168 | tf_op jit(solution)/shard_map/psum | solution.py:51
  545.6 3.1 broadcast_multiply_fusion
  (7 shorter events, 0.1 us)
Async XLA Ops:
  8.7 19.5 %all-to-all-start.1 = ((bf16[16,1,128]{2,1,0:T(2,128)(2,1)}), bf16[16,1,128]{2,1,0:T(2,128)(2,1)S(1)}, u32[]{:S(2)}, u32[]{:S(2)}) async-start(bf16[16,1,128]{2,1,0:T(2,128)(2,1)} %copy.20), calls=%async_computation.1 | async-start | bytes 16384 | tf_op jit(solution)/shard_map/all_to_all | solution.py:46
  28.2 41.3 %all-to-all-start.2 = ((bf16[16,256,256]{2,1,0:T(8,128)(2,1)}), bf16[16,256,256]{2,1,0:T(8,128)(2,1)S(1)}, u32[]{:S(2)}, u32[]{:S(2)}) async-start(bf16[16,256,256]{2,1,0:T(8,128)(2,1)} %scatter_fusion.2), calls=%async_computation.2 | async-start | bytes 4194304 | tf_op jit(solution)/shard_map/all_to_all | solution.py:45
  69.5 377.1 %all-to-all-start = ((bf16[16,3072,256]{2,1,0:T(8,128)(2,1)}), bf16[16,3072,256]{2,1,0:T(8,128)(2,1)}, u32[]{:S(2)}, u32[]{:S(2)}) async-start(bf16[16,3072,256]{2,1,0:T(8,128)(2,1)} %scatter_fusion), calls=%async_computation | async-start | bytes 50331648 | tf_op jit(solution)/shard_map/all_to_all | solution.py:44
  76.7 468.9 %all-reduce.2.cloned.1.call-start = ((), (), s32[]{:S(2)}) async-start(), calls=%async_computation.3 | async-start | bytes 4194304 | tf_op jit(solution)/shard_map/psum | solution.py:51
Sparse Core Ops, SparseCore 0:
  481.3 64.2 all-reduce.1
where the time goes:
time: 556 us
  waiting for transfers between devices  434 us (78%)
  local copies, waits for them, and re-layouts  55.9 us (10%)
  starting transfers between devices  22.6 us (4%)
  matrix products  19.9 us (4%)
  between operations  13.5 us (2%)
  other arithmetic  9.96 us (2%)
    all_to_all x1, waiting for transfers between devices, on_device(): lax.all_to_all(vec_buf, 'win', split_axis=0, concat_axis=0, tiled=True)  369 us
    psum x1, waiting for transfers between devices, on_device(): total = lax.psum(partial_value, 'space')  64.4 us
    scatter x1, local copies, waits for them, and re-layouts, on_device(): jnp.zeros((nblocks,) + modes.shape[1:], jnp.bfloat16).at[dest].set(modes)  25.7 us
    dot_general x1, matrix products, batch_grams(): jnp.einsum('wps,wpt->wst', resid, resid, preferred_element_type=jnp.float32)  19.9 us
    gather x2, local copies, waits for them, and re-layouts, on_device(): partial_value = batch_grams(snapshots, got_vec[source], got_coef[source])  15.2 us
  transfers between devices with their start and end apart: 4, of which 2 were waited for; matrix products, arithmetic and copies ran while one was open for 8% of the time, Pallas kernels for 0%

commit v1 on v0

v1 whole, which is shorter than its diff:
```python
import functools

import jax
import jax.numpy as jnp
from jax import lax
from jax.experimental import pallas as pl
from jax.experimental.pallas import tpu as pltpu
from jax.sharding import PartitionSpec as P

K = 128
S = 256
WIN_DEV = 8
NCH = 1
TP = 1536


def coefficients(amp_re, amp_im, growth, freq, mode_count):
    steps = jnp.arange(S).astype(jnp.float32)
    live = (jnp.arange(K, dtype=jnp.int32)[None, :] < mode_count[:, None]).astype(jnp.float32)
    decay = jnp.exp(growth[:, :, None] * steps) * live[:, :, None]
    angle = freq[:, :, None] * steps
    cosine = jnp.cos(angle)
    sine = jnp.sin(angle)
    real_part = (amp_re[:, :, None] * cosine - amp_im[:, :, None] * sine) * decay
    imag_part = (amp_re[:, :, None] * sine + amp_im[:, :, None] * cosine) * decay
    stacked = jnp.stack([real_part, -imag_part], axis=2)
    return stacked.reshape(amp_re.shape[0], 2 * K, S).astype(jnp.bfloat16)


def gram_kernel(src_ref, s_ref, m_ref, c_ref, o_ref):
    t = pl.program_id(1)

    @pl.when(t == 0)
    def _():
        o_ref[...] = jnp.zeros_like(o_ref)

    s = s_ref[0].astype(jnp.float32)
    recon = jnp.dot(m_ref[0], c_ref[0], preferred_element_type=jnp.float32)
    r = (s - recon).astype(jnp.bfloat16)
    half = S // 2
    dims = (((0,), (0,)), ((), ()))
    top = lax.dot_general(r[:, :half], r, dims, preferred_element_type=jnp.float32)
    low = lax.dot_general(r[:, half:], r[:, half:], dims, preferred_element_type=jnp.float32)
    o_ref[0, :, : 2 * half] += top
    o_ref[0, :, 2 * half :] += low


def chunk_gram(source, snapshots, got, coef, chunk):
    nw, _, s = snapshots.shape
    rows = got.shape[1]
    tp = min(TP, rows)
    nt = rows // tp
    base = chunk * nt
    return pl.pallas_call(
        gram_kernel,
        grid_spec=pltpu.PrefetchScalarGridSpec(
            num_scalar_prefetch=1,
            grid=(nw, nt),
            in_specs=[
                pl.BlockSpec((1, tp, s), lambda p, t, src: (p, base + t, 0)),
                pl.BlockSpec((1, tp, s), lambda p, t, src: (src[p], t, 0)),
                pl.BlockSpec((1, s, s), lambda p, t, src: (p, 0, 0)),
            ],
            out_specs=pl.BlockSpec((1, s // 2, 3 * s // 2), lambda p, t, src: (p, 0, 0)),
        ),
        out_shape=jax.ShapeDtypeStruct((nw, s // 2, 3 * s // 2), jnp.float32),
        compiler_params=pltpu.CompilerParams(
            dimension_semantics=("arbitrary", "arbitrary"),
            vmem_limit_bytes=48 * 1024 * 1024,
        ),
        cost_estimate=pl.CostEstimate(
            flops=int(nw * rows * s * s * 2 * 1.75),
            bytes_accessed=int(nw * rows * s * 2 * 2),
            transcendentals=0,
        ),
    )(source, snapshots, got, coef)


def on_device(snapshots, modes, amp_re, amp_im, growth, freq, mode_count, slot_window):
    nblocks = lax.axis_size("win")
    me = lax.axis_index("win")
    nw, rows, s = snapshots.shape
    points_all = rows * lax.axis_size("space")

    dest = slot_window // WIN_DEV
    hit = dest[None, :] == jnp.arange(nblocks, dtype=jnp.int32)[:, None]
    pick = jnp.sum(jnp.where(hit, jnp.arange(nw, dtype=jnp.int32)[None, :], 0), axis=1)

    cp = rows // NCH
    gots = []
    for k in range(NCH):
        part = modes[:, k * cp : (k + 1) * cp, :]
        sendbuf = jnp.take(part, pick, axis=0, mode="clip")
        gots.append(lax.all_to_all(sendbuf, "win", split_axis=0, concat_axis=0, tiled=True))

    extra = jnp.zeros((nw, K), jnp.float32)
    extra = extra.at[:, 0].set(mode_count.astype(jnp.float32))
    extra = extra.at[:, 1].set(slot_window.astype(jnp.float32))
    packed = jnp.concatenate([amp_re, amp_im, growth, freq, extra], axis=1)
    packed_all = lax.all_gather(packed, "win", axis=0, tiled=True)
    sw_all = packed_all[:, 4 * K + 1].astype(jnp.int32)
    wins = me * WIN_DEV + jnp.arange(nw, dtype=jnp.int32)
    slot_ids = jnp.arange(packed_all.shape[0], dtype=jnp.int32)
    slot = jnp.sum(jnp.where(sw_all[None, :] == wins[:, None], slot_ids[None, :], 0), axis=1)
    source = slot // WIN_DEV
    sel = jnp.take(packed_all, slot, axis=0, mode="clip")
    coef = coefficients(
        sel[:, 0:K],
        sel[:, K : 2 * K],
        sel[:, 2 * K : 3 * K],
        sel[:, 3 * K : 4 * K],
        sel[:, 4 * K].astype(jnp.int32),
    )

    part_sum = None
    for k in range(NCH):
        g = chunk_gram(source, snapshots, gots[k], coef, k)
        part_sum = g if part_sum is None else part_sum + g
    total = lax.psum(part_sum, "space") / points_all
    half = s // 2
    top = total[:, :, :s]
    mid = total[:, :, half:s]
    low = total[:, :, s:]
    bottom = jnp.concatenate([jnp.swapaxes(mid, 1, 2), low], axis=2)
    return jnp.concatenate([top, bottom], axis=1)


def solution(mesh):
    return jax.shard_map(
        on_device,
        mesh=mesh,
        in_specs=(
            P("win", "space", None),
            P("win", "space", None),
            P("win", None),
            P("win", None),
            P("win", None),
            P("win", None),
            P("win"),
            P("win"),
        ),
        out_specs=P("win", None, None),
        check_vma=False,
    )
```

time: 556 us -> 517 us (0.930)
  local copies, waits for them, and re-layouts: 55.9 us -> 20 us
  blocking collectives: 0 us -> 25.5 us
  Pallas kernels: 0 us -> 21.9 us
  matrix products: 19.9 us -> 0 us
  waiting for transfers between devices: 434 us -> 416 us
  starting transfers between devices: 22.6 us -> 5.57 us
    scatter x3 -> x2, local copies, waits for them, and re-layouts: 29.4 us -> 0.09 us  [the longest x1 0.09 us: on_device(): extra = extra.at[:, 1].set(slot_window.astype(jnp.float32))]
    all_gather x0 -> x1, blocking collectives: none -> 25.5 us  [on_device(): packed_all = lax.all_gather(packed, 'win', axis=0, tiled=True)]
    pallas_call x0 -> x1, Pallas kernels: none -> 21.9 us  [chunk_gram(): pl.pallas_call(gram_kernel, grid_spec=pltpu.PrefetchScalarGridSpec(num_sc...]
    dot_general x1 -> x0, matrix products: 19.9 us -> none  [batch_grams(): jnp.einsum('wps,wpt->wst', resid, resid, preferred_element_type=jnp.float32)]
    all_to_all x3 -> x1, waiting for transfers between devices: 369 us -> 351 us  [on_device(): lax.all_to_all(sendbuf, 'win', split_axis=0, concat_axis=0, tiled=True)]
    all_to_all x3 -> x1, starting transfers between devices: 22.5 us -> 5.53 us  [on_device(): lax.all_to_all(sendbuf, 'win', split_axis=0, concat_axis=0, tiled=True)]
    broadcast_in_dim x3 -> x0, local copies, waits for them, and re-layouts: 9.87 us -> none  [the longest x1 8.34 us: on_device(): jnp.zeros((nblocks,) + modes.shape[1:], jnp.bfloat16).at[dest].set(modes)]
  transfers between devices with their start and end apart: 4 -> 2, of which waited for: 2 -> 2; matrix products, arithmetic and copies ran while one was open for 8% -> 1% of each run, Pallas kernels for 0% -> 0%
where the time goes in v1:
time: 517 us; the launch traced here: 516 us
  waiting for transfers between devices  416 us (80%)
  blocking collectives  25.5 us (5%)
  Pallas kernels  21.9 us (4%)
  local copies, waits for them, and re-layouts  20 us (4%)
  between operations  13.5 us (3%)
  other arithmetic  13 us (3%)
  starting transfers between devices  5.57 us (1%)
    all_to_all x1, waiting for transfers between devices, on_device(): lax.all_to_all(sendbuf, 'win', split_axis=0, concat_axis=0, tiled=True)  351 us
    psum x1, waiting for transfers between devices, on_device(): total = lax.psum(part_sum, 'space') / points_all  65.5 us
    all_gather x1, blocking collectives, on_device(): packed_all = lax.all_gather(packed, 'win', axis=0, tiled=True)  25.5 us
    pallas_call x1, Pallas kernels, chunk_gram(): pl.pallas_call(gram_kernel, grid_spec=pltpu.PrefetchScalarGridSpec(num_sc...  21.9 us
    gather x1, local copies, waits for them, and re-layouts, on_device(): sendbuf = jnp.take(part, pick, axis=0, mode='clip')  14.5 us
  transfers between devices with their start and end apart: 2, of which 2 were waited for; matrix products, arithmetic and copies ran while one was open for 1% of the time, Pallas kernels for 0%

profile of v1, /device:TPU:0, one launch (start us, length us, event | category | flops | bytes accessed | tf_op | source)
XLA Modules:
  0.0 515.7 jit_solution(4576334866344996725)
XLA Ops:
  6.5 0.6 compare_reduce_fusion.1
  7.2 0.7 compare_reduce_fusion
  7.9 0.7 constant_dynamic-update-slice_fusion.4
  8.6 1.3 fusion.14
  9.9 0.1 copy.18
  10.0 0.7 and_select_fusion
  10.6 1.3 fusion.15
  12.0 0.1 copy.19
  12.1 0.7 constant_dynamic-update-slice_fusion.3
  12.8 0.7 constant_dynamic-update-slice_fusion.2
  13.4 0.7 constant_dynamic-update-slice_fusion.1
  14.1 0.1 scatter.9
  14.2 25.5 %all_gather.3 = f32[128,640]{1,0:T(8,128)S(1)} all-gather(f32[8,640]{1,0:T(8,128)S(1)} %constant_dynamic-update-slice_fusion), channel_id=1, replica_groups=mesh['space'=8,'win'=16] {'win'}, dimensions={0}, use_global_device_ids=true | all-gather | bytes 348160 | tf_op jit(solution)/shard_map/all_gather | solution.py:100
  39.7 0.2 fusion.11
  39.9 0.1 select_reduce_fusion
  40.0 0.2 select_reduce_fusion.1
  40.2 14.5 %gather_fusion = bf16[16,3072,256]{2,1,0:T(8,128)(2,1)} fusion(bf16[8,3072,256]{2,1,0:T(8,128)(2,1)} %param.13, s32[1024]{0:T(1024)S(1)} %get-tuple-element.38), kind=kCustom, calls=%fused_computation | custom fusion | bytes 50331712 | tf_op jit(solution)/shard_map/jit(_take)/gather | solution.py:93
  54.7 5.5 %all-to-all-start = ((bf16[16,3072,256]{2,1,0:T(8,128)(2,1)}), bf16[16,3072,256]{2,1,0:T(8,128)(2,1)}, u32[]{:S(2)}, u32[]{:S(2)}) async-start(bf16[16,3072,256]{2,1,0:T(8,128)(2,1)} %gather_fusion), calls=%async_computation | async-start | bytes 50331648 | tf_op jit(solution)/shard_map/all_to_all | solution.py:94
  60.3 0.0 all-reduce.3.cloned.1.call-start
  60.3 0.6 gather_fusion.1
  60.9 0.1 fusion.12
  61.0 0.1 fusion.13
  61.1 4.5 fusion.6
  65.6 0.1 pad_maximum_fusion
  65.7 1.1 copy.20
  66.8 0.4 convert_element_type.49.c_ref
  67.3 350.7 %all-to-all-done.m_ref = bf16[16,3072,256]{2,1,0:T(8,128)(2,1)} async-done(((bf16[16,3072,256]{2,1,0:T(8,128)(2,1)}), bf16[16,3072,256]{2,1,0:T(8,128)(2,1)}, u32[]{:S(2)}, u32[]{:S(2)}) %all-to-all-start) | async-done | bytes 25165856 | tf_op jit(solution)/shard_map/all_to_all | solution.py:94
  418.0 21.9 %shard_map.82 = f32[8,128,384]{2,1,0:T(8,128)} custom-call(s32[8]{0:T(128)S(1)} %and_select_fusion.1.src_ref, bf16[8,3072,256]{2,1,0:T(8,128)(2,1)} %s_ref.1, bf16[16,3072,256]{2,1,0:T(8,128)(2,1)} %all-to-all-done.m_ref, bf16[8,256,256]{2,1,0:T(8,128)(2,1)S(1)} %convert_element_type.49.c_ref), custom_call_target="tpu_custom_call" | custom-call | flops 5637144576 | bytes 25165824 | tf_op jit(solution)/shard_map/pallas_call | solution.py:54
  439.9 0.0 all-reduce.3.cloned.1.call-update
  439.9 65.5 %all-reduce.3.cloned.1.call-done = f32[8,128,384]{2,1,0:T(8,128)} async-done(((f32[8,128,384]{2,1,0:T(8,128)}), f32[8,128,384]{2,1,0:T(8,128)}) %all-reduce.3.cloned.1.call-update) | async-done | bytes 1572880 | tf_op jit(solution)/shard_map/psum | solution.py:119
  505.4 1.5 broadcast_multiply_fusion
  506.9 0.1 fusion.16
  507.1 0.1 slice.75
  507.2 0.2 copy.22
  507.4 1.5 maximum_maximum_fusion
  (7 shorter events, 0.0 us)
Async XLA Ops:
  54.7 363.3 %all-to-all-start = ((bf16[16,3072,256]{2,1,0:T(8,128)(2,1)}), bf16[16,3072,256]{2,1,0:T(8,128)(2,1)}, u32[]{:S(2)}, u32[]{:S(2)}) async-start(bf16[16,3072,256]{2,1,0:T(8,128)(2,1)} %gather_fusion), calls=%async_computation | async-start | bytes 50331648 | tf_op jit(solution)/shard_map/all_to_all | solution.py:94
  60.3 445.1 %all-reduce.3.cloned.1.call-start = ((), (), s32[]{:S(2)}) async-start(), calls=%async_computation.1 | async-start | bytes 3145728 | tf_op jit(solution)/shard_map/psum | solution.py:119
Sparse Core Ops, SparseCore 0:
  440.0 65.3 all-reduce.2

commit v2 on v1

--- a/solution.py
+++ b/solution.py
@@ -1,5 +1,3 @@
-import functools
-
 import jax
 import jax.numpy as jnp
 from jax import lax
@@ -7,10 +5,11 @@
 from jax.experimental.pallas import tpu as pltpu
 from jax.sharding import PartitionSpec as P
 
+
 K = 128
 S = 256
 WIN_DEV = 8
-NCH = 1
+NCH = 2
 TP = 1536
 
 
@@ -101,9 +100,10 @@
     sw_all = packed_all[:, 4 * K + 1].astype(jnp.int32)
     wins = me * WIN_DEV + jnp.arange(nw, dtype=jnp.int32)
     slot_ids = jnp.arange(packed_all.shape[0], dtype=jnp.int32)
-    slot = jnp.sum(jnp.where(sw_all[None, :] == wins[:, None], slot_ids[None, :], 0), axis=1)
+    match = sw_all[None, :] == wins[:, None]
+    slot = jnp.sum(jnp.where(match, slot_ids[None, :], 0), axis=1)
     source = slot // WIN_DEV
-    sel = jnp.take(packed_all, slot, axis=0, mode="clip")
+    sel = jnp.sum(jnp.where(match[:, :, None], packed_all[None, :, :], 0.0), axis=1)
     coef = coefficients(
         sel[:, 0:K],
         sel[:, K : 2 * K],

time: 517 us -> 531 us (1.027)
  waiting for transfers between devices: 416 us -> 242 us
  blocking collectives: 25.5 us -> 196 us
  local copies, waits for them, and re-layouts: 20 us -> 30.5 us
  starting transfers between devices: 5.57 us -> 13.2 us
    all_to_all x1 -> x2, waiting for transfers between devices: 351 us -> 178 us  [on_device(): lax.all_to_all(sendbuf, 'win', split_axis=0, concat_axis=0, tiled=True)]
    all_gather x1, blocking collectives: 25.5 us -> 196 us  [on_device(): packed_all = lax.all_gather(packed, 'win', axis=0, tiled=True)]
    slice x0 -> x1, local copies, waits for them, and re-layouts: none -> 10.2 us  [on_device(): part = modes[:, k * cp:(k + 1) * cp, :]]
    all_to_all x1 -> x2, starting transfers between devices: 5.53 us -> 13.2 us  [on_device(): lax.all_to_all(sendbuf, 'win', split_axis=0, concat_axis=0, tiled=True)]
    gather x1 -> x2, local copies, waits for them, and re-layouts: 14.5 us -> 18.2 us  [on_device(): sendbuf = jnp.take(part, pick, axis=0, mode='clip')]
    pallas_call x1 -> x2, Pallas kernels: 21.9 us -> 22.3 us  [chunk_gram(): pl.pallas_call(gram_kernel, grid_spec=pltpu.PrefetchScalarGridSpec(num_sc...]
  transfers between devices with their start and end apart: 2 -> 3, of which waited for: 2 -> 2; matrix products, arithmetic and copies ran while one was open for 1% -> 4% of each run, Pallas kernels for 0% -> 2%
where the time goes in v2:
time: 531 us
  waiting for transfers between devices  242 us (46%)
  blocking collectives  196 us (37%)
  local copies, waits for them, and re-layouts  30.5 us (6%)
  Pallas kernels  22.3 us (4%)
  between operations  13.6 us (3%)
  starting transfers between devices  13.2 us (2%)
  other arithmetic  12.6 us (2%)
    all_gather x1, blocking collectives, on_device(): packed_all = lax.all_gather(packed, 'win', axis=0, tiled=True)  196 us
    all_to_all x2, waiting for transfers between devices, on_device(): lax.all_to_all(sendbuf, 'win', split_axis=0, concat_axis=0, tiled=True)  178 us
    psum x1, waiting for transfers between devices, on_device(): total = lax.psum(part_sum, 'space') / points_all  64 us
    pallas_call x2, Pallas kernels, chunk_gram(): pl.pallas_call(gram_kernel, grid_spec=pltpu.PrefetchScalarGridSpec(num_sc...  22.3 us
    gather x2, local copies, waits for them, and re-layouts, on_device(): sendbuf = jnp.take(part, pick, axis=0, mode='clip')  18.2 us
    all_to_all x2, starting transfers between devices, on_device(): lax.all_to_all(sendbuf, 'win', split_axis=0, concat_axis=0, tiled=True)  13.2 us
  transfers between devices with their start and end apart: 3, of which 2 were waited for; matrix products, arithmetic and copies ran while one was open for 4% of the time, Pallas kernels for 2%

profile of v2, /device:TPU:0, one launch (start us, length us, event | category | flops | bytes accessed | tf_op | source)
XLA Modules:
  0.0 530.6 jit_solution(4164633742154171265)
XLA Ops:
  6.5 0.0 copy-start.5
  6.5 10.2 %fusion.16 = (bf16[8,1536,256]{2,1,0:T(8,128)(2,1)}, bf16[8,1536,256]{2,1,0:T(8,128)(2,1)}) fusion(bf16[8,3072,256]{2,1,0:T(8,128)(2,1)} %param.13), kind=kLoop, calls=%fused_computation.53 | loop fusion | bytes 25165824 | tf_op jit(solution)/shard_map/slice | solution.py:91
  16.8 0.0 copy-done.5
  16.8 0.1 select_reduce_fusion.1
  16.9 9.0 %gather_fusion = bf16[16,1536,256]{2,1,0:T(8,128)(2,1)} fusion(bf16[8,1536,256]{2,1,0:T(8,128)(2,1)} %get-tuple-element.30, s32[1024]{0:T(1024)S(1)} %pad_clamp_fusion), kind=kCustom, calls=%fused_computation | custom fusion | bytes 25165888 | tf_op jit(solution)/shard_map/jit(_take)/gather | solution.py:92
  25.9 8.2 %all-to-all-start = ((bf16[16,1536,256]{2,1,0:T(8,128)(2,1)}), bf16[16,1536,256]{2,1,0:T(8,128)(2,1)}, u32[]{:S(2)}, u32[]{:S(2)}) async-start(bf16[16,1536,256]{2,1,0:T(8,128)(2,1)} %gather_fusion), calls=%async_computation | async-start | bytes 25165824 | tf_op jit(solution)/shard_map/all_to_all | solution.py:93
  34.1 9.2 %gather_fusion.1 = bf16[16,1536,256]{2,1,0:T(8,128)(2,1)} fusion(bf16[8,1536,256]{2,1,0:T(8,128)(2,1)} %get-tuple-element.29, s32[1024]{0:T(1024)S(1)} %pad_clamp_fusion), kind=kCustom, calls=%fused_computation.1 | custom fusion | bytes 25165888 | tf_op jit(solution)/shard_map/jit(_take)/gather | solution.py:92
  43.3 0.0 copy-start.4
  43.3 0.0 copy-start
  43.3 0.0 copy-start.1
  43.3 0.0 copy-start.2
  43.3 0.0 copy-start.3
  43.3 177.8 %all-to-all-done.m_ref = bf16[16,1536,256]{2,1,0:T(8,128)(2,1)} async-done(((bf16[16,1536,256]{2,1,0:T(8,128)(2,1)}), bf16[16,1536,256]{2,1,0:T(8,128)(2,1)}, u32[]{:S(2)}, u32[]{:S(2)}) %all-to-all-start) | async-done | bytes 12582944 | tf_op jit(solution)/shard_map/all_to_all | solution.py:93
  221.2 5.0 all-to-all-start.1
  226.2 0.0 all-reduce.3.cloned.1.call-start
  226.2 0.6 compare_reduce_fusion.1
  226.9 0.0 copy-done.4
  226.9 0.6 fusion.14
  227.5 0.6 compare_reduce_fusion
  228.2 0.6 fusion.15
  228.9 0.1 copy.35
  228.9 0.0 copy-done
  228.9 0.0 copy-done.1
  228.9 0.0 copy-done.2
  229.0 0.0 copy-done.3
  229.0 196.4 %all_gather.3 = f32[128,640]{1,0:T(8,128)S(1)} all-gather(f32[8,640]{1,0:T(8,128)S(1)} %constant_dynamic-update-slice_fusion), channel_id=1, replica_groups=mesh['space'=8,'win'=16] {'win'}, dimensions={0}, use_global_device_ids=true | all-gather | bytes 348160 | tf_op jit(solution)/shard_map/all_gather | solution.py:99
  425.4 0.2 fusion.11
  425.6 0.1 broadcast_compare_fusion
  425.7 0.3 select_reduce_fusion
  426.0 0.1 fusion.12
  426.1 0.1 fusion.13
  426.2 4.5 fusion.6
  430.7 0.1 pad_maximum_fusion
  430.8 1.1 copy.36
  431.9 0.4 convert_element_type.49.c_ref
  432.3 0.2 select_reduce_fusion.2
  432.5 11.2 %shard_map.82 = f32[8,128,384]{2,1,0:T(8,128)S(1)} custom-call(s32[8]{0:T(128)S(1)} %and_select_fusion.1.src_ref, bf16[8,3072,256]{2,1,0:T(8,128)(2,1)} %s_ref.3, bf16[16,1536,256]{2,1,0:T(8,128)(2,1)} %all-to-all-done.m_ref, bf16[8,256,256]{2,1,0:T(8,128)(2,1)S(1)} %convert_element_type.49.c_ref), custom_call_target="tpu_custom_call" | custom-call | flops 2818572288 | bytes 12582912 | tf_op jit(solution)/shard_map/pallas_call | solution.py:53
  443.7 0.0 all-to-all-done.1.m_ref
  443.7 11.2 %shard_map.83 = f32[8,128,384]{2,1,0:T(8,128)S(1)} custom-call(s32[8]{0:T(128)S(1)} %and_select_fusion.1.src_ref, bf16[8,3072,256]{2,1,0:T(8,128)(2,1)} %s_ref.3, bf16[16,1536,256]{2,1,0:T(8,128)(2,1)} %all-to-all-done.1.m_ref, bf16[8,256,256]{2,1,0:T(8,128)(2,1)S(1)} %convert_element_type.49.c_ref), custom_call_target="tpu_custom_call" | custom-call | flops 2818572288 | bytes 12582912 | tf_op jit(solution)/shard_map/pallas_call | solution.py:53
  454.9 1.3 add.36
  456.2 0.0 all-reduce.3.cloned.1.call-update
  456.2 64.0 %all-reduce.3.cloned.1.call-done = f32[8,128,384]{2,1,0:T(8,128)} async-done(((f32[8,128,384]{2,1,0:T(8,128)}), f32[8,128,384]{2,1,0:T(8,128)}) %all-reduce.3.cloned.1.call-update) | async-done | bytes 1572880 | tf_op jit(solution)/shard_map/psum | solution.py:119
  520.2 1.5 broadcast_multiply_fusion
  521.8 0.1 fusion.17
  521.9 0.1 slice.83
  522.0 0.2 copy.38
  522.2 1.5 maximum_maximum_fusion
  (13 shorter events, 0.1 us)
Async XLA Ops:
  6.5 10.2 %copy-start.5 = (s32[8]{0:T(128)S(1)}, s32[8]{0:T(128)}, u32[]{:S(2)}) copy-start(s32[8]{0:T(128)} %param.19) | copy-start | bytes 100
  25.9 195.2 %all-to-all-start = ((bf16[16,1536,256]{2,1,0:T(8,128)(2,1)}), bf16[16,1536,256]{2,1,0:T(8,128)(2,1)}, u32[]{:S(2)}, u32[]{:S(2)}) async-start(bf16[16,1536,256]{2,1,0:T(8,128)(2,1)} %gather_fusion), calls=%async_computation | async-start | bytes 25165824 | tf_op jit(solution)/shard_map/all_to_all | solution.py:93
  43.3 183.6 %copy-start.4 = (s32[8]{0:T(128)S(1)}, s32[8]{0:T(128)}, u32[]{:S(2)}) copy-start(s32[8]{0:T(128)} %param.18) | copy-start | bytes 100
  43.3 185.6 %copy-start = (f32[8,128]{1,0:T(8,128)S(1)}, f32[8,128]{1,0:T(8,128)}, u32[]{:S(2)}) copy-start(f32[8,128]{1,0:T(8,128)} %param.14) | copy-start | bytes 12292
  43.3 185.6 %copy-start.1 = (f32[8,128]{1,0:T(8,128)S(1)}, f32[8,128]{1,0:T(8,128)}, u32[]{:S(2)}) copy-start(f32[8,128]{1,0:T(8,128)} %param.15) | copy-start | bytes 12292
  43.3 185.6 %copy-start.2 = (f32[8,128]{1,0:T(8,128)S(1)}, f32[8,128]{1,0:T(8,128)}, u32[]{:S(2)}) copy-start(f32[8,128]{1,0:T(8,128)} %param.16) | copy-start | bytes 12292
  43.3 185.6 %copy-start.3 = (f32[8,128]{1,0:T(8,128)S(1)}, f32[8,128]{1,0:T(8,128)}, u32[]{:S(2)}) copy-start(f32[8,128]{1,0:T(8,128)} %param.17) | copy-start | bytes 12292
  221.2 222.5 %all-to-all-start.1 = ((bf16[16,1536,256]{2,1,0:T(8,128)(2,1)}), bf16[16,1536,256]{2,1,0:T(8,128)(2,1)}, u32[]{:S(2)}, u32[]{:S(2)}) async-start(bf16[16,1536,256]{2,1,0:T(8,128)(2,1)} %gather_fusion.1), calls=%async_computation.1 | async-start | bytes 25165824 | tf_op jit(solution)/shard_map/all_to_all | solution.py:93
  226.2 294.1 %all-reduce.3.cloned.1.call-start = ((), (), s32[]{:S(2)}) async-start(), calls=%async_computation.2 | async-start | bytes 3145728 | tf_op jit(solution)/shard_map/psum | solution.py:119
Sparse Core Ops, SparseCore 0:
  456.3 63.8 all-reduce.2

commit v3 on v2

--- a/solution.py
+++ b/solution.py
@@ -75,6 +75,30 @@
     )(source, snapshots, got, coef)
 
 
+def copy_kernel(pick_ref, m_ref, o_ref):
+    o_ref[...] = m_ref[...]
+
+
+def send_buffer(pick, modes, chunk, rows):
+    nb = pick.shape[0]
+    s = modes.shape[2]
+    tq = min(TP, rows)
+    nt = rows // tq
+    base = chunk * nt
+    return pl.pallas_call(
+        copy_kernel,
+        grid_spec=pltpu.PrefetchScalarGridSpec(
+            num_scalar_prefetch=1,
+            grid=(nb, nt),
+            in_specs=[pl.BlockSpec((1, tq, s), lambda b, t, pk: (pk[b], base + t, 0))],
+            out_specs=pl.BlockSpec((1, tq, s), lambda b, t, pk: (b, t, 0)),
+        ),
+        out_shape=jax.ShapeDtypeStruct((nb, rows, s), modes.dtype),
+        compiler_params=pltpu.CompilerParams(dimension_semantics=("arbitrary", "arbitrary")),
+        cost_estimate=pl.CostEstimate(flops=0, bytes_accessed=2 * nb * rows * s * 2, transcendentals=0),
+    )(pick, modes)
+
+
 def on_device(snapshots, modes, amp_re, amp_im, growth, freq, mode_count, slot_window):
     nblocks = lax.axis_size("win")
     me = lax.axis_index("win")
@@ -88,8 +112,7 @@
     cp = rows // NCH
     gots = []
     for k in range(NCH):
-        part = modes[:, k * cp : (k + 1) * cp, :]
-        sendbuf = jnp.take(part, pick, axis=0, mode="clip")
+        sendbuf = send_buffer(pick, modes, k, cp)
         gots.append(lax.all_to_all(sendbuf, "win", split_axis=0, concat_axis=0, tiled=True))
 
     extra = jnp.zeros((nw, K), jnp.float32)

time: 531 us -> 530 us (level)
  Pallas kernels: 22.3 us -> 52.1 us
  local copies, waits for them, and re-layouts: 30.5 us -> 2.06 us
  waiting for transfers between devices: 242 us -> 236 us
    pallas_call x0 -> x2, Pallas kernels: none -> 29.8 us  [send_buffer(): pl.pallas_call(copy_kernel, grid_spec=pltpu.PrefetchScalarGridSpec(num_sc...]
    gather x2 -> x0, local copies, waits for them, and re-layouts: 18.2 us -> none  [on_device(): sendbuf = jnp.take(part, pick, axis=0, mode='clip')]
    slice x1 -> x0, local copies, waits for them, and re-layouts: 10.2 us -> none  [on_device(): part = modes[:, k * cp:(k + 1) * cp, :]]
    all_to_all x2, waiting for transfers between devices: 178 us -> 172 us  [on_device(): lax.all_to_all(sendbuf, 'win', split_axis=0, concat_axis=0, tiled=True)]
  transfers between devices with their start and end apart: 3 -> 3, of which waited for: 2 -> 2; matrix products, arithmetic and copies ran while one was open for 4% -> 2% of each run, Pallas kernels for 2% -> 5%
where the time goes in v3:
time: 530 us; the launch traced here: 528 us
  waiting for transfers between devices  236 us (45%)
  blocking collectives  196 us (37%)
  Pallas kernels  52.1 us (10%)
  starting transfers between devices  14.2 us (3%)
  other arithmetic  13.7 us (3%)
  between operations  13.6 us (3%)
    all_gather x1, blocking collectives, on_device(): packed_all = lax.all_gather(packed, 'win', axis=0, tiled=True)  196 us
    all_to_all x2, waiting for transfers between devices, on_device(): lax.all_to_all(sendbuf, 'win', split_axis=0, concat_axis=0, tiled=True)  172 us
    psum x1, waiting for transfers between devices, on_device(): total = lax.psum(part_sum, 'space') / points_all  64 us
    pallas_call x2, Pallas kernels, send_buffer(): pl.pallas_call(copy_kernel, grid_spec=pltpu.PrefetchScalarGridSpec(num_sc...  29.8 us
    pallas_call x2, Pallas kernels, chunk_gram(): pl.pallas_call(gram_kernel, grid_spec=pltpu.PrefetchScalarGridSpec(num_sc...  22.3 us
    all_to_all x2, starting transfers between devices, on_device(): lax.all_to_all(sendbuf, 'win', split_axis=0, concat_axis=0, tiled=True)  14.2 us
  transfers between devices with their start and end apart: 3, of which 2 were waited for; matrix products, arithmetic and copies ran while one was open for 2% of the time, Pallas kernels for 5%

profile of v3, /device:TPU:0, one launch (start us, length us, event | category | flops | bytes accessed | tf_op | source)
XLA Modules:
  0.0 528.4 jit_solution(8803938247553945447)
XLA Ops:
  6.5 0.7 and_select_fusion
  7.2 0.6 select_reduce_fusion.1.pick_ref
  7.8 14.9 %shard_map.84 = bf16[16,1536,256]{2,1,0:T(8,128)(2,1)} custom-call(s32[16]{0:T(128)} %select_reduce_fusion.1.pick_ref, bf16[8,3072,256]{2,1,0:T(8,128)(2,1)} %m_ref.3), custom_call_target="tpu_custom_call" | custom-call | bytes 25165824 | tf_op jit(solution)/shard_map/pallas_call | solution.py:88
  22.7 9.2 %all-to-all-start.1 = ((bf16[16,1536,256]{2,1,0:T(8,128)(2,1)}), bf16[16,1536,256]{2,1,0:T(8,128)(2,1)}, u32[]{:S(2)}, u32[]{:S(2)}) async-start(bf16[16,1536,256]{2,1,0:T(8,128)(2,1)} %shard_map.84), calls=%async_computation.1 | async-start | bytes 25165824 | tf_op jit(solution)/shard_map/all_to_all | solution.py:116
  31.9 14.9 %shard_map.82 = bf16[16,1536,256]{2,1,0:T(8,128)(2,1)} custom-call(s32[16]{0:T(128)} %select_reduce_fusion.1.pick_ref, bf16[8,3072,256]{2,1,0:T(8,128)(2,1)} %m_ref.3), custom_call_target="tpu_custom_call" | custom-call | bytes 25165824 | tf_op jit(solution)/shard_map/pallas_call | solution.py:88
  46.8 0.0 copy-start.4
  46.8 0.0 copy-start.5
  46.8 0.0 copy-start
  46.8 0.0 copy-start.1
  46.8 0.0 copy-start.2
  46.8 0.0 copy-start.3
  46.8 172.1 %all-to-all-done.1.m_ref = bf16[16,1536,256]{2,1,0:T(8,128)(2,1)} async-done(((bf16[16,1536,256]{2,1,0:T(8,128)(2,1)}), bf16[16,1536,256]{2,1,0:T(8,128)(2,1)}, u32[]{:S(2)}, u32[]{:S(2)}) %all-to-all-start.1) | async-done | bytes 12582944 | tf_op jit(solution)/shard_map/all_to_all | solution.py:116
  219.0 5.0 all-to-all-start
  224.0 0.0 all-reduce.3.cloned.1.call-start
  224.0 0.6 compare_reduce_fusion.1
  224.7 0.0 copy-done.4
  224.7 0.6 fusion.14
  225.3 0.6 compare_reduce_fusion
  226.0 0.0 copy-done.5
  226.0 0.6 fusion.15
  226.7 0.1 copy.35
  226.7 0.0 copy-done
  226.7 0.0 copy-done.1
  226.8 0.0 copy-done.2
  226.8 0.0 copy-done.3
  226.8 196.4 %all_gather.3 = f32[128,640]{1,0:T(8,128)S(1)} all-gather(f32[8,640]{1,0:T(8,128)S(1)} %constant_dynamic-update-slice_fusion), channel_id=1, replica_groups=mesh['space'=8,'win'=16] {'win'}, dimensions={0}, use_global_device_ids=true | all-gather | bytes 348160 | tf_op jit(solution)/shard_map/all_gather | solution.py:122
  423.2 0.2 fusion.11
  423.4 0.1 broadcast_compare_fusion
  423.5 0.3 select_reduce_fusion
  423.8 0.1 fusion.12
  423.9 0.1 fusion.13
  424.0 4.5 fusion.6
  428.5 0.1 pad_maximum_fusion
  428.6 1.1 copy.36
  429.7 0.4 convert_element_type.49.c_ref
  430.1 0.2 select_reduce_fusion.2
  430.3 11.2 %shard_map.85 = f32[8,128,384]{2,1,0:T(8,128)S(1)} custom-call(s32[8]{0:T(128)S(1)} %and_select_fusion.1.src_ref, bf16[8,3072,256]{2,1,0:T(8,128)(2,1)} %s_ref.3, bf16[16,1536,256]{2,1,0:T(8,128)(2,1)} %all-to-all-done.1.m_ref, bf16[8,256,256]{2,1,0:T(8,128)(2,1)S(1)} %convert_element_type.49.c_ref), custom_call_target="tpu_custom_call" | custom-call | flops 2818572288 | bytes 12582912 | tf_op jit(solution)/shard_map/pallas_call | solution.py:53
  441.5 0.0 all-to-all-done.m_ref
  441.5 11.2 %shard_map.83 = f32[8,128,384]{2,1,0:T(8,128)S(1)} custom-call(s32[8]{0:T(128)S(1)} %and_select_fusion.1.src_ref, bf16[8,3072,256]{2,1,0:T(8,128)(2,1)} %s_ref.3, bf16[16,1536,256]{2,1,0:T(8,128)(2,1)} %all-to-all-done.m_ref, bf16[8,256,256]{2,1,0:T(8,128)(2,1)S(1)} %convert_element_type.49.c_ref), custom_call_target="tpu_custom_call" | custom-call | flops 2818572288 | bytes 12582912 | tf_op jit(solution)/shard_map/pallas_call | solution.py:53
  452.7 1.3 add.36
  454.0 0.0 all-reduce.3.cloned.1.call-update
  454.0 64.0 %all-reduce.3.cloned.1.call-done = f32[8,128,384]{2,1,0:T(8,128)} async-done(((f32[8,128,384]{2,1,0:T(8,128)}), f32[8,128,384]{2,1,0:T(8,128)}) %all-reduce.3.cloned.1.call-update) | async-done | bytes 1572880 | tf_op jit(solution)/shard_map/psum | solution.py:142
  518.0 1.5 broadcast_multiply_fusion
  519.6 0.1 slice.71
  519.7 0.1 fusion.16
  519.8 0.2 copy.38
  520.0 1.5 maximum_maximum_fusion
  (11 shorter events, 0.1 us)
Async XLA Ops:
  22.7 196.2 %all-to-all-start.1 = ((bf16[16,1536,256]{2,1,0:T(8,128)(2,1)}), bf16[16,1536,256]{2,1,0:T(8,128)(2,1)}, u32[]{:S(2)}, u32[]{:S(2)}) async-start(bf16[16,1536,256]{2,1,0:T(8,128)(2,1)} %shard_map.84), calls=%async_computation.1 | async-start | bytes 25165824 | tf_op jit(solution)/shard_map/all_to_all | solution.py:116
  46.8 177.8 %copy-start.4 = (s32[8]{0:T(128)S(1)}, s32[8]{0:T(128)}, u32[]{:S(2)}) copy-start(s32[8]{0:T(128)} %param.18) | copy-start | bytes 100
  46.8 179.2 %copy-start.5 = (s32[8]{0:T(128)S(1)}, s32[8]{0:T(128)}, u32[]{:S(2)}) copy-start(s32[8]{0:T(128)} %param.19) | copy-start | bytes 100
  46.8 179.9 %copy-start = (f32[8,128]{1,0:T(8,128)S(1)}, f32[8,128]{1,0:T(8,128)}, u32[]{:S(2)}) copy-start(f32[8,128]{1,0:T(8,128)} %param.14) | copy-start | bytes 12292
  46.8 179.9 %copy-start.1 = (f32[8,128]{1,0:T(8,128)S(1)}, f32[8,128]{1,0:T(8,128)}, u32[]{:S(2)}) copy-start(f32[8,128]{1,0:T(8,128)} %param.15) | copy-start | bytes 12292
  46.8 179.9 %copy-start.2 = (f32[8,128]{1,0:T(8,128)S(1)}, f32[8,128]{1,0:T(8,128)}, u32[]{:S(2)}) copy-start(f32[8,128]{1,0:T(8,128)} %param.16) | copy-start | bytes 12292
  46.8 179.9 %copy-start.3 = (f32[8,128]{1,0:T(8,128)S(1)}, f32[8,128]{1,0:T(8,128)}, u32[]{:S(2)}) copy-start(f32[8,128]{1,0:T(8,128)} %param.17) | copy-start | bytes 12292
  219.0 222.5 %all-to-all-start = ((bf16[16,1536,256]{2,1,0:T(8,128)(2,1)}), bf16[16,1536,256]{2,1,0:T(8,128)(2,1)}, u32[]{:S(2)}, u32[]{:S(2)}) async-start(bf16[16,1536,256]{2,1,0:T(8,128)(2,1)} %shard_map.82), calls=%async_computation | async-start | bytes 25165824 | tf_op jit(solution)/shard_map/all_to_all | solution.py:116
  224.0 294.1 %all-reduce.3.cloned.1.call-start = ((), (), s32[]{:S(2)}) async-start(), calls=%async_computation.2 | async-start | bytes 3145728 | tf_op jit(solution)/shard_map/psum | solution.py:142
Sparse Core Ops, SparseCore 0:
  454.1 63.8 all-reduce.2

commit v4 on v3

--- a/solution.py
+++ b/solution.py
@@ -9,7 +9,7 @@
 K = 128
 S = 256
 WIN_DEV = 8
-NCH = 2
+NCH = 1
 TP = 1536
 
 
@@ -112,7 +112,10 @@
     cp = rows // NCH
     gots = []
     for k in range(NCH):
-        sendbuf = send_buffer(pick, modes, k, cp)
+        if NCH == 1:
+            sendbuf = jnp.take(modes, pick, axis=0, mode="clip")
+        else:
+            sendbuf = send_buffer(pick, modes, k, cp)
         gots.append(lax.all_to_all(sendbuf, "win", split_axis=0, concat_axis=0, tiled=True))
 
     extra = jnp.zeros((nw, K), jnp.float32)

time: 530 us -> 523 us (0.987)
  blocking collectives: 196 us -> 386 us
  waiting for transfers between devices: 236 us -> 63.5 us
  Pallas kernels: 52.1 us -> 21.9 us
  local copies, waits for them, and re-layouts: 2.06 us -> 16.6 us
  starting transfers between devices: 14.2 us -> 8.39 us
    all_gather x1, blocking collectives: 196 us -> 386 us  [on_device(): packed_all = lax.all_gather(packed, 'win', axis=0, tiled=True)]
    all_to_all x2 -> x1, waiting for transfers between devices: 172 us -> 0.01 us  [on_device(): lax.all_to_all(sendbuf, 'win', split_axis=0, concat_axis=0, tiled=True)]
    pallas_call x2 -> x0, Pallas kernels: 29.8 us -> none  [send_buffer(): pl.pallas_call(copy_kernel, grid_spec=pltpu.PrefetchScalarGridSpec(num_sc...]
    gather x0 -> x1, local copies, waits for them, and re-layouts: none -> 14.5 us  [on_device(): sendbuf = jnp.take(modes, pick, axis=0, mode='clip')]
    all_to_all x2 -> x1, starting transfers between devices: 14.2 us -> 8.35 us  [on_device(): lax.all_to_all(sendbuf, 'win', split_axis=0, concat_axis=0, tiled=True)]
    pallas_call x2 -> x1, Pallas kernels: 22.3 us -> 21.9 us  [chunk_gram(): pl.pallas_call(gram_kernel, grid_spec=pltpu.PrefetchScalarGridSpec(num_sc...]
  transfers between devices with their start and end apart: 3 -> 2, of which waited for: 2 -> 1; matrix products, arithmetic and copies ran while one was open for 2% -> 2% of each run, Pallas kernels for 5% -> 0%
where the time goes in v4:
time: 523 us; the launch traced here: 522 us
  blocking collectives  386 us (74%)
  waiting for transfers between devices  63.5 us (12%)
  Pallas kernels  21.9 us (4%)
  local copies, waits for them, and re-layouts  16.6 us (3%)
  between operations  13.6 us (3%)
  other arithmetic  11.9 us (2%)
  starting transfers between devices  8.39 us (2%)
    all_gather x1, blocking collectives, on_device(): packed_all = lax.all_gather(packed, 'win', axis=0, tiled=True)  386 us
    psum x1, waiting for transfers between devices, on_device(): total = lax.psum(part_sum, 'space') / points_all  63.4 us
    pallas_call x1, Pallas kernels, chunk_gram(): pl.pallas_call(gram_kernel, grid_spec=pltpu.PrefetchScalarGridSpec(num_sc...  21.9 us
    gather x1, local copies, waits for them, and re-layouts, on_device(): sendbuf = jnp.take(modes, pick, axis=0, mode='clip')  14.5 us
  transfers between devices with their start and end apart: 2, of which 1 were waited for; matrix products, arithmetic and copies ran while one was open for 2% of the time, Pallas kernels for 0%

profile of v4, /device:TPU:0, one launch (start us, length us, event | category | flops | bytes accessed | tf_op | source)
XLA Modules:
  0.0 522.2 jit_solution(11734565620746687245)
XLA Ops:
  6.5 0.7 and_select_fusion
  7.2 0.1 select_reduce_fusion.1
  7.3 14.5 %gather_fusion = bf16[16,3072,256]{2,1,0:T(8,128)(2,1)} fusion(bf16[8,3072,256]{2,1,0:T(8,128)(2,1)} %param.13, s32[1024]{0:T(1024)S(1)} %pad_clamp_fusion), kind=kCustom, calls=%fused_computation | custom fusion | bytes 50331712 | tf_op jit(solution)/shard_map/jit(_take)/gather | solution.py:116
  21.8 0.0 copy-start.4
  21.8 0.0 copy-start.5
  21.8 0.0 copy-start
  21.8 0.0 copy-start.1
  21.8 0.0 copy-start.2
  21.9 0.0 copy-start.3
  21.9 8.3 %all-to-all-start = ((bf16[16,3072,256]{2,1,0:T(8,128)(2,1)}), bf16[16,3072,256]{2,1,0:T(8,128)(2,1)}, u32[]{:S(2)}, u32[]{:S(2)}) async-start(bf16[16,3072,256]{2,1,0:T(8,128)(2,1)} %gather_fusion), calls=%async_computation | async-start | bytes 50331648 | tf_op jit(solution)/shard_map/all_to_all | solution.py:119
  30.2 0.0 all-reduce.3.cloned.1.call-start
  30.3 0.6 compare_reduce_fusion.1
  30.9 0.0 copy-done.4
  30.9 0.6 fusion.14
  31.6 0.6 compare_reduce_fusion
  32.2 0.0 copy-done.5
  32.2 0.6 fusion.15
  32.9 0.1 copy.35
  33.0 0.0 copy-done
  33.0 0.0 copy-done.1
  33.0 0.0 copy-done.2
  33.0 0.0 copy-done.3
  33.1 386.3 %all_gather.3 = f32[128,640]{1,0:T(8,128)S(1)} all-gather(f32[8,640]{1,0:T(8,128)S(1)} %constant_dynamic-update-slice_fusion), channel_id=1, replica_groups=mesh['space'=8,'win'=16] {'win'}, dimensions={0}, use_global_device_ids=true | all-gather | bytes 348160 | tf_op jit(solution)/shard_map/all_gather | solution.py:125
  419.4 0.2 fusion.11
  419.5 0.1 broadcast_compare_fusion
  419.6 0.3 select_reduce_fusion
  419.9 0.1 fusion.12
  420.0 0.1 fusion.13
  420.1 4.5 fusion.6
  424.6 0.1 pad_maximum_fusion
  424.7 1.1 copy.36
  425.8 0.4 convert_element_type.49.c_ref
  426.3 0.2 select_reduce_fusion.2
  426.5 0.0 all-to-all-done.m_ref
  426.5 21.9 %shard_map.82 = f32[8,128,384]{2,1,0:T(8,128)} custom-call(s32[8]{0:T(128)S(1)} %and_select_fusion.1.src_ref, bf16[8,3072,256]{2,1,0:T(8,128)(2,1)} %s_ref.1, bf16[16,3072,256]{2,1,0:T(8,128)(2,1)} %all-to-all-done.m_ref, bf16[8,256,256]{2,1,0:T(8,128)(2,1)S(1)} %convert_element_type.49.c_ref), custom_call_target="tpu_custom_call" | custom-call | flops 5637144576 | bytes 25165824 | tf_op jit(solution)/shard_map/pallas_call | solution.py:53
  448.4 0.0 all-reduce.3.cloned.1.call-update
  448.4 63.4 %all-reduce.3.cloned.1.call-done = f32[8,128,384]{2,1,0:T(8,128)} async-done(((f32[8,128,384]{2,1,0:T(8,128)}), f32[8,128,384]{2,1,0:T(8,128)}) %all-reduce.3.cloned.1.call-update) | async-done | bytes 1572880 | tf_op jit(solution)/shard_map/psum | solution.py:145
  511.8 1.5 broadcast_multiply_fusion
  513.4 0.1 fusion.16
  513.5 0.1 slice.73
  513.6 0.2 copy.38
  513.8 1.5 maximum_maximum_fusion
  (12 shorter events, 0.1 us)
Async XLA Ops:
  21.8 9.1 %copy-start.4 = (s32[8]{0:T(128)S(1)}, s32[8]{0:T(128)}, u32[]{:S(2)}) copy-start(s32[8]{0:T(128)} %param.18) | copy-start | bytes 100
  21.8 10.4 %copy-start.5 = (s32[8]{0:T(128)S(1)}, s32[8]{0:T(128)}, u32[]{:S(2)}) copy-start(s32[8]{0:T(128)} %param.19) | copy-start | bytes 100
  21.8 11.1 %copy-start = (f32[8,128]{1,0:T(8,128)S(1)}, f32[8,128]{1,0:T(8,128)}, u32[]{:S(2)}) copy-start(f32[8,128]{1,0:T(8,128)} %param.14) | copy-start | bytes 12292
  21.8 11.1 %copy-start.1 = (f32[8,128]{1,0:T(8,128)S(1)}, f32[8,128]{1,0:T(8,128)}, u32[]{:S(2)}) copy-start(f32[8,128]{1,0:T(8,128)} %param.15) | copy-start | bytes 12292
  21.8 11.2 %copy-start.2 = (f32[8,128]{1,0:T(8,128)S(1)}, f32[8,128]{1,0:T(8,128)}, u32[]{:S(2)}) copy-start(f32[8,128]{1,0:T(8,128)} %param.16) | copy-start | bytes 12292
  21.9 11.2 %copy-start.3 = (f32[8,128]{1,0:T(8,128)S(1)}, f32[8,128]{1,0:T(8,128)}, u32[]{:S(2)}) copy-start(f32[8,128]{1,0:T(8,128)} %param.17) | copy-start | bytes 12292
  21.9 404.6 %all-to-all-start = ((bf16[16,3072,256]{2,1,0:T(8,128)(2,1)}), bf16[16,3072,256]{2,1,0:T(8,128)(2,1)}, u32[]{:S(2)}, u32[]{:S(2)}) async-start(bf16[16,3072,256]{2,1,0:T(8,128)(2,1)} %gather_fusion), calls=%async_computation | async-start | bytes 50331648 | tf_op jit(solution)/shard_map/all_to_all | solution.py:119
  30.2 481.6 %all-reduce.3.cloned.1.call-start = ((), (), s32[]{:S(2)}) async-start(), calls=%async_computation.1 | async-start | bytes 3145728 | tf_op jit(solution)/shard_map/psum | solution.py:145
Sparse Core Ops, SparseCore 0:
  448.5 63.2 all-reduce.2

commit v5 on v3

--- a/solution.py
+++ b/solution.py
@@ -1,3 +1,5 @@
+import functools
+
 import jax
 import jax.numpy as jnp
 from jax import lax
@@ -9,7 +11,7 @@
 K = 128
 S = 256
 WIN_DEV = 8
-NCH = 2
+NCH = 1
 TP = 1536
 
 
@@ -99,6 +101,75 @@
     )(pick, modes)
 
 
+def exchange_kernel(sb_ref, pk_ref, out_ref, pall_ref, send_sem, recv_sem, psend_sem, precv_sem, own_sem):
+    n = out_ref.shape[0]
+    me = lax.axis_index("win")
+    sp = lax.axis_index("space")
+    mesh_id = pl.DeviceIdType.MESH
+
+    barrier = pltpu.get_barrier_semaphore()
+    for k in range(1, n):
+        peer = lax.rem(me + k, n)
+        pl.semaphore_signal(barrier, inc=1, device_id=(sp, peer), device_id_type=mesh_id)
+    pl.semaphore_wait(barrier, n - 1)
+
+    own = pltpu.make_async_copy(sb_ref.at[me], out_ref.at[me], own_sem.at[0])
+    own.start()
+    ownp = pltpu.make_async_copy(pk_ref, pall_ref.at[me], own_sem.at[1])
+    ownp.start()
+    copies = []
+    for k in range(1, n):
+        peer = lax.rem(me + k, n)
+        pc = pltpu.make_async_remote_copy(
+            src_ref=pk_ref,
+            dst_ref=pall_ref.at[me],
+            send_sem=psend_sem.at[k],
+            recv_sem=precv_sem.at[k],
+            device_id=(sp, peer),
+            device_id_type=mesh_id,
+        )
+        pc.start()
+        copies.append(pc)
+    for k in range(1, n):
+        peer = lax.rem(me + k, n)
+        c = pltpu.make_async_remote_copy(
+            src_ref=sb_ref.at[peer],
+            dst_ref=out_ref.at[me],
+            send_sem=send_sem.at[k],
+            recv_sem=recv_sem.at[k],
+            device_id=(sp, peer),
+            device_id_type=mesh_id,
+        )
+        c.start()
+        copies.append(c)
+    own.wait()
+    ownp.wait()
+    for c in copies:
+        c.wait()
+
+
+def exchange(sendbuf, packed):
+    n = sendbuf.shape[0]
+    any_spec = pl.BlockSpec(memory_space=pl.ANY)
+    return pl.pallas_call(
+        exchange_kernel,
+        in_specs=[any_spec, any_spec],
+        out_specs=[any_spec, any_spec],
+        out_shape=[
+            jax.ShapeDtypeStruct(sendbuf.shape, sendbuf.dtype),
+            jax.ShapeDtypeStruct((n,) + packed.shape, packed.dtype),
+        ],
+        scratch_shapes=[
+            pltpu.SemaphoreType.DMA((n,)),
+            pltpu.SemaphoreType.DMA((n,)),
+            pltpu.SemaphoreType.DMA((n,)),
+            pltpu.SemaphoreType.DMA((n,)),
+            pltpu.SemaphoreType.DMA((2,)),
+        ],
+        compiler_params=pltpu.CompilerParams(collective_id=0, has_side_effects=True),
+    )(sendbuf, packed)
+
+
 def on_device(snapshots, modes, amp_re, amp_im, growth, freq, mode_count, slot_window):
     nblocks = lax.axis_size("win")
     me = lax.axis_index("win")
@@ -109,17 +180,14 @@
     hit = dest[None, :] == jnp.arange(nblocks, dtype=jnp.int32)[:, None]
     pick = jnp.sum(jnp.where(hit, jnp.arange(nw, dtype=jnp.int32)[None, :], 0), axis=1)
 
-    cp = rows // NCH
-    gots = []
-    for k in range(NCH):
-        sendbuf = send_buffer(pick, modes, k, cp)
-        gots.append(lax.all_to_all(sendbuf, "win", split_axis=0, concat_axis=0, tiled=True))
-
     extra = jnp.zeros((nw, K), jnp.float32)
     extra = extra.at[:, 0].set(mode_count.astype(jnp.float32))
     extra = extra.at[:, 1].set(slot_window.astype(jnp.float32))
     packed = jnp.concatenate([amp_re, amp_im, growth, freq, extra], axis=1)
-    packed_all = lax.all_gather(packed, "win", axis=0, tiled=True)
+    sendbuf = jnp.take(modes, pick, axis=0, mode="clip")
+    got, packed_all = exchange(sendbuf, packed)
+    packed_all = packed_all.reshape((-1, packed.shape[1]))
+    gots = [got]
     sw_all = packed_all[:, 4 * K + 1].astype(jnp.int32)
     wins = me * WIN_DEV + jnp.arange(nw, dtype=jnp.int32)
     slot_ids = jnp.arange(packed_all.shape[0], dtype=jnp.int32)

time: 530 us -> 600 us (1.13)
  Pallas kernels: 52.1 us -> 460 us
  blocking collectives: 196 us -> 0 us
  waiting for transfers between devices: 236 us -> 91.6 us
  local copies, waits for them, and re-layouts: 2.06 us -> 18.2 us
  starting transfers between devices: 14.2 us -> 0.01 us
    pallas_call x2 -> x1, Pallas kernels: 29.8 us -> 439 us  [exchange(): pl.pallas_call(exchange_kernel, in_specs=[any_spec, any_spec], out_specs=...]
    all_gather x1 -> x0, blocking collectives: 196 us -> none  [on_device(): packed_all = lax.all_gather(packed, 'win', axis=0, tiled=True)]
    all_to_all x2 -> x0, waiting for transfers between devices: 172 us -> none  [on_device(): lax.all_to_all(sendbuf, 'win', split_axis=0, concat_axis=0, tiled=True)]
    psum x1, waiting for transfers between devices: 64 us -> 91.6 us  [on_device(): total = lax.psum(part_sum, 'space') / points_all]
    gather x0 -> x1, local copies, waits for them, and re-layouts: none -> 14.6 us  [on_device(): sendbuf = jnp.take(modes, pick, axis=0, mode='clip')]
    all_to_all x2 -> x0, starting transfers between devices: 14.2 us -> none  [on_device(): lax.all_to_all(sendbuf, 'win', split_axis=0, concat_axis=0, tiled=True)]
    pallas_call x2 -> x1, Pallas kernels: 22.3 us -> 21.9 us  [chunk_gram(): pl.pallas_call(gram_kernel, grid_spec=pltpu.PrefetchScalarGridSpec(num_sc...]
  transfers between devices with their start and end apart: 3 -> 1, of which waited for: 2 -> 1; matrix products, arithmetic and copies ran while one was open for 2% -> 0% of each run, Pallas kernels for 5% -> 0%
where the time goes in v5:
time: 600 us; the launch traced here: 599 us
  Pallas kernels  460 us (77%)
  waiting for transfers between devices  91.6 us (15%)
  local copies, waits for them, and re-layouts  18.2 us (3%)
  other arithmetic  15.1 us (3%)
  between operations  13.5 us (2%)
    pallas_call x1, Pallas kernels, exchange(): pl.pallas_call(exchange_kernel, in_specs=[any_spec, any_spec], out_specs=...  439 us
    psum x1, waiting for transfers between devices, on_device(): total = lax.psum(part_sum, 'space') / points_all  91.6 us
    pallas_call x1, Pallas kernels, chunk_gram(): pl.pallas_call(gram_kernel, grid_spec=pltpu.PrefetchScalarGridSpec(num_sc...  21.9 us
    gather x1, local copies, waits for them, and re-layouts, on_device(): sendbuf = jnp.take(modes, pick, axis=0, mode='clip')  14.6 us
  transfers between devices with their start and end apart: 1, of which 1 were waited for; matrix products, arithmetic and copies ran while one was open for 0% of the time, Pallas kernels for 0%

profile of v5, /device:TPU:0, one launch (start us, length us, event | category | flops | bytes accessed | tf_op | source)
XLA Modules:
  0.0 598.9 jit_solution(3856379346350588574)
XLA Ops:
  6.5 0.0 all-reduce.3.cloned.1.call-start
  6.5 0.6 compare_reduce_fusion.1
  7.2 0.7 compare_reduce_fusion
  7.9 0.7 and_select_fusion.1
  8.6 0.1 select_reduce_fusion.2
  8.7 0.7 constant_dynamic-update-slice_fusion.4
  9.3 1.3 fusion.13
  10.6 0.1 copy.25
  10.7 1.3 fusion.14
  12.1 0.1 copy.26
  12.2 0.0 copy-start.1
  12.2 0.0 copy-start.2
  12.2 0.0 copy-start.3
  12.2 14.6 %gather_fusion = bf16[16,3072,256]{2,1,0:T(8,128)(2,1)} fusion(bf16[8,3072,256]{2,1,0:T(8,128)(2,1)} %param.13, s32[1024]{0:T(1024)S(1)} %pad_clamp_fusion), kind=kCustom, calls=%fused_computation | custom fusion | bytes 50331712 | tf_op jit(solution)/shard_map/jit(_take)/gather | solution.py:187
  26.8 0.0 copy-done.1
  26.8 0.0 copy-done.2
  26.8 0.0 copy-done.3
  26.8 0.1 scatter.9
  26.9 0.0 copy-start
  26.9 0.6 copy-done
  27.6 438.6 %shard_map.82 = (bf16[16,3072,256]{2,1,0:T(8,128)(2,1)}, f32[16,8,640]{2,1,0:T(8,128)}) custom-call(bf16[16,3072,256]{2,1,0:T(8,128)(2,1)} %gather_fusion, f32[8,640]{1,0:T(8,128)} %copy-done), custom_call_target="tpu_custom_call" | custom-call | tf_op jit(solution)/shard_map/pallas_call | solution.py:154
  466.2 0.9 slice_convert_fusion
  467.1 0.1 copy.32
  467.1 0.1 broadcast_compare_fusion
  467.2 1.3 select_reduce_fusion
  468.5 0.1 fusion.11
  468.6 0.2 select_reduce_fusion.1
  468.8 0.1 fusion.12
  468.9 4.5 fusion.6
  473.4 0.1 pad_maximum_fusion
  473.5 1.1 copy.28
  474.6 0.4 convert_element_type.49.c_ref
  475.1 21.9 %shard_map.83 = f32[8,128,384]{2,1,0:T(8,128)} custom-call(s32[8]{0:T(128)S(1)} %and_select_fusion.src_ref, bf16[8,3072,256]{2,1,0:T(8,128)(2,1)} %s_ref.1, bf16[16,3072,256]{2,1,0:T(8,128)(2,1)} %get-tuple-element.32.m_ref, bf16[8,256,256]{2,1,0:T(8,128)(2,1)S(1)} %convert_element_type.49.c_ref), custom_call_target="tpu_custom_call" | custom-call | flops 5637144576 | bytes 25165824 | tf_op jit(solution)/shard_map/pallas_call | solution.py:55
  497.0 0.0 all-reduce.3.cloned.1.call-update
  497.0 91.6 %all-reduce.3.cloned.1.call-done = f32[8,128,384]{2,1,0:T(8,128)} async-done(((f32[8,128,384]{2,1,0:T(8,128)}), f32[8,128,384]{2,1,0:T(8,128)}) %all-reduce.3.cloned.1.call-update) | async-done | bytes 1572880 | tf_op jit(solution)/shard_map/psum | solution.py:210
  588.6 1.5 broadcast_multiply_fusion
  590.2 0.1 fusion.15
  590.3 0.1 slice.73
  590.4 0.2 copy.31
  590.6 1.5 maximum_maximum_fusion
  (10 shorter events, 0.0 us)
Async XLA Ops:
  6.5 582.1 %all-reduce.3.cloned.1.call-start = ((), (), s32[]{:S(2)}) async-start(), calls=%async_computation | async-start | bytes 3145728 | tf_op jit(solution)/shard_map/psum | solution.py:210
  12.2 14.6 %copy-start.1 = (f32[8,128]{1,0:T(8,128)S(1)}, f32[8,128]{1,0:T(8,128)}, u32[]{:S(2)}) copy-start(f32[8,128]{1,0:T(8,128)} %param.15) | copy-start | bytes 12292
  12.2 14.6 %copy-start.2 = (f32[8,128]{1,0:T(8,128)S(1)}, f32[8,128]{1,0:T(8,128)}, u32[]{:S(2)}) copy-start(f32[8,128]{1,0:T(8,128)} %param.16) | copy-start | bytes 12292
  12.2 14.6 %copy-start.3 = (f32[8,128]{1,0:T(8,128)S(1)}, f32[8,128]{1,0:T(8,128)}, u32[]{:S(2)}) copy-start(f32[8,128]{1,0:T(8,128)} %param.17) | copy-start | bytes 12292
  26.9 0.6 copy-start
Sparse Core Ops, SparseCore 0:
  497.1 91.4 all-reduce.2

commit v6 on v2

--- a/solution.py
+++ b/solution.py
@@ -86,17 +86,19 @@
     pick = jnp.sum(jnp.where(hit, jnp.arange(nw, dtype=jnp.int32)[None, :], 0), axis=1)
 
     cp = rows // NCH
+    modes_r = modes.reshape(nw, NCH, cp, s)
     gots = []
     for k in range(NCH):
-        part = modes[:, k * cp : (k + 1) * cp, :]
-        sendbuf = jnp.take(part, pick, axis=0, mode="clip")
+        sendbuf = modes_r[pick, k]
         gots.append(lax.all_to_all(sendbuf, "win", split_axis=0, concat_axis=0, tiled=True))
 
     extra = jnp.zeros((nw, K), jnp.float32)
     extra = extra.at[:, 0].set(mode_count.astype(jnp.float32))
     extra = extra.at[:, 1].set(slot_window.astype(jnp.float32))
     packed = jnp.concatenate([amp_re, amp_im, growth, freq, extra], axis=1)
-    packed_all = lax.all_gather(packed, "win", axis=0, tiled=True)
+    spread = jnp.zeros((nblocks,) + packed.shape, jnp.float32)
+    spread = lax.dynamic_update_slice(spread, packed[None], (me, 0, 0))
+    packed_all = lax.psum(spread, "win").reshape((-1, packed.shape[1]))
     sw_all = packed_all[:, 4 * K + 1].astype(jnp.int32)
     wins = me * WIN_DEV + jnp.arange(nw, dtype=jnp.int32)
     slot_ids = jnp.arange(packed_all.shape[0], dtype=jnp.int32)

time: 531 us -> 552 us (1.040)
  waiting for transfers between devices: 242 us -> 462 us
  blocking collectives: 196 us -> 0 us
  local copies, waits for them, and re-layouts: 30.5 us -> 24.7 us
    psum x0 -> x1, waiting for transfers between devices: none -> 223 us  [on_device(): packed_all = lax.psum(spread, 'win').reshape((-1, packed.shape[1]))]
    all_gather x1 -> x0, blocking collectives: 196 us -> none  [on_device(): packed_all = lax.all_gather(packed, 'win', axis=0, tiled=True)]
    slice x1 -> x0, local copies, waits for them, and re-layouts: 10.2 us -> none  [on_device(): part = modes[:, k * cp:(k + 1) * cp, :]]
  transfers between devices with their start and end apart: 3 -> 4, of which waited for: 2 -> 3; matrix products, arithmetic and copies ran while one was open for 4% -> 4% of each run, Pallas kernels for 2% -> 2%
where the time goes in v6:
time: 552 us; the launch traced here: 551 us
  waiting for transfers between devices  462 us (84%)
  local copies, waits for them, and re-layouts  24.7 us (4%)
  Pallas kernels  22.3 us (4%)
  other arithmetic  15.1 us (3%)
  between operations  13.7 us (2%)
  starting transfers between devices  13.3 us (2%)
    psum x1, waiting for transfers between devices, on_device(): packed_all = lax.psum(spread, 'win').reshape((-1, packed.shape[1]))  223 us
    all_to_all x2, waiting for transfers between devices, on_device(): lax.all_to_all(sendbuf, 'win', split_axis=0, concat_axis=0, tiled=True)  176 us
    psum x1, waiting for transfers between devices, on_device(): total = lax.psum(part_sum, 'space') / points_all  63.5 us
    pallas_call x2, Pallas kernels, chunk_gram(): pl.pallas_call(gram_kernel, grid_spec=pltpu.PrefetchScalarGridSpec(num_sc...  22.3 us
    gather x2, local copies, waits for them, and re-layouts, on_device(): sendbuf = modes_r[pick, k]  21.9 us
    all_to_all x2, starting transfers between devices, on_device(): lax.all_to_all(sendbuf, 'win', split_axis=0, concat_axis=0, tiled=True)  13.2 us
  transfers between devices with their start and end apart: 4, of which 3 were waited for; matrix products, arithmetic and copies ran while one was open for 4% of the time, Pallas kernels for 2%

profile of v6, /device:TPU:0, one launch (start us, length us, event | category | flops | bytes accessed | tf_op | source)
XLA Modules:
  0.0 551.5 jit_solution(3956518010167696287)
XLA Ops:
  6.5 0.7 and_select_fusion
  7.2 0.1 select_reduce_fusion.1
  7.3 11.0 %gather_fusion.1 = bf16[16,1536,256]{2,1,0:T(8,128)(2,1)} fusion(bf16[8,2,1536,256]{3,2,1,0:T(8,128)(2,1)} %bitcast.19, s32[16]{0:T(128)S(1)} %get-tuple-element.37), kind=kCustom, calls=%fused_computation.1 | custom fusion | bytes 25165952 | tf_op jit(solution)/shard_map/gather | solution.py:92
  18.3 8.2 %all-to-all-start.1 = ((bf16[16,1536,256]{2,1,0:T(8,128)(2,1)}), bf16[16,1536,256]{2,1,0:T(8,128)(2,1)}, u32[]{:S(2)}, u32[]{:S(2)}) async-start(bf16[16,1536,256]{2,1,0:T(8,128)(2,1)} %gather_fusion.1), calls=%async_computation.1 | async-start | bytes 25165824 | tf_op jit(solution)/shard_map/all_to_all | solution.py:93
  26.5 10.9 %gather_fusion = bf16[16,1536,256]{2,1,0:T(8,128)(2,1)} fusion(bf16[8,2,1536,256]{3,2,1,0:T(8,128)(2,1)} %bitcast.20, s32[16]{0:T(128)S(1)} %get-tuple-element.38), kind=kCustom, calls=%fused_computation | custom fusion | bytes 25165952 | tf_op jit(solution)/shard_map/gather | solution.py:92
  37.4 0.0 copy-start.5
  37.4 0.0 copy-start.6
  37.4 0.0 copy-start.1
  37.4 0.0 copy-start.2
  37.5 0.0 copy-start.3
  37.5 0.0 copy-start.4
  37.5 176.1 %all-to-all-done.1.m_ref = bf16[16,1536,256]{2,1,0:T(8,128)(2,1)} async-done(((bf16[16,1536,256]{2,1,0:T(8,128)(2,1)}), bf16[16,1536,256]{2,1,0:T(8,128)(2,1)}, u32[]{:S(2)}, u32[]{:S(2)}) %all-to-all-start.1) | async-done | bytes 12582944 | tf_op jit(solution)/shard_map/all_to_all | solution.py:93
  213.6 5.0 all-to-all-start
  218.6 0.0 all-reduce.6.cloned.1.call-start
  218.6 0.6 compare_reduce_fusion.1
  219.2 0.0 copy-done.5
  219.3 0.6 fusion.14
  219.9 0.6 compare_reduce_fusion
  220.6 0.0 copy-done.6
  220.6 0.6 fusion.15
  221.3 0.1 copy.50
  221.3 0.0 copy-done.1
  221.3 0.0 copy-done.2
  221.3 0.0 copy-done.3
  221.4 0.0 copy-done.4
  221.4 0.0 copy-start
  221.5 0.7 copy-done
  222.2 0.0 all-reduce.6.cloned.1.call-update
  222.2 0.0 all-reduce.8.cloned.1.call-start
  222.3 222.8 %all-reduce.6.cloned.1.call-done = f32[128,640]{1,0:T(8,128)} async-done(((f32[128,640]{1,0:T(8,128)}), f32[128,640]{1,0:T(8,128)}) %all-reduce.6.cloned.1.call-update) | async-done | bytes 327696 | tf_op jit(solution)/shard_map/psum | solution.py:101
  445.0 1.0 fusion.11
  446.1 0.1 broadcast_compare_fusion
  446.1 1.3 select_reduce_fusion
  447.4 0.1 fusion.12
  447.5 0.1 fusion.13
  447.6 4.5 fusion.6
  452.1 0.1 pad_maximum_fusion
  452.2 1.1 copy.51
  453.3 0.4 convert_element_type.49.c_ref
  453.8 0.2 select_reduce_fusion.2
  454.0 11.2 %shard_map.83 = f32[8,128,384]{2,1,0:T(8,128)S(1)} custom-call(s32[8]{0:T(128)S(1)} %and_select_fusion.1.src_ref, bf16[8,3072,256]{2,1,0:T(8,128)(2,1)} %s_ref.3, bf16[16,1536,256]{2,1,0:T(8,128)(2,1)} %all-to-all-done.1.m_ref, bf16[8,256,256]{2,1,0:T(8,128)(2,1)S(1)} %convert_element_type.49.c_ref), custom_call_target="tpu_custom_call" | custom-call | flops 2818572288 | bytes 12582912 | tf_op jit(solution)/shard_map/pallas_call | solution.py:53
  465.1 0.0 all-to-all-done.m_ref
  465.1 11.2 %shard_map.82 = f32[8,128,384]{2,1,0:T(8,128)S(1)} custom-call(s32[8]{0:T(128)S(1)} %and_select_fusion.1.src_ref, bf16[8,3072,256]{2,1,0:T(8,128)(2,1)} %s_ref.3, bf16[16,1536,256]{2,1,0:T(8,128)(2,1)} %all-to-all-done.m_ref, bf16[8,256,256]{2,1,0:T(8,128)(2,1)S(1)} %convert_element_type.49.c_ref), custom_call_target="tpu_custom_call" | custom-call | flops 2818572288 | bytes 12582912 | tf_op jit(solution)/shard_map/pallas_call | solution.py:53
  476.3 1.3 add.58
  477.6 0.0 all-reduce.8.cloned.1.call-update
  477.6 63.5 %all-reduce.8.cloned.1.call-done = f32[8,128,384]{2,1,0:T(8,128)} async-done(((f32[8,128,384]{2,1,0:T(8,128)}), f32[8,128,384]{2,1,0:T(8,128)}) %all-reduce.8.cloned.1.call-update) | async-done | bytes 1572880 | tf_op jit(solution)/shard_map/psum | solution.py:121
  541.2 1.5 broadcast_multiply_fusion
  542.7 0.1 slice.75
  542.8 0.1 fusion.19
  542.9 0.2 copy.53
  543.1 1.5 maximum_maximum_fusion
  (14 shorter events, 0.1 us)
Async XLA Ops:
  18.3 195.2 %all-to-all-start.1 = ((bf16[16,1536,256]{2,1,0:T(8,128)(2,1)}), bf16[16,1536,256]{2,1,0:T(8,128)(2,1)}, u32[]{:S(2)}, u32[]{:S(2)}) async-start(bf16[16,1536,256]{2,1,0:T(8,128)(2,1)} %gather_fusion.1), calls=%async_computation.1 | async-start | bytes 25165824 | tf_op jit(solution)/shard_map/all_to_all | solution.py:93
  37.4 181.8 %copy-start.5 = (s32[8]{0:T(128)S(1)}, s32[8]{0:T(128)}, u32[]{:S(2)}) copy-start(s32[8]{0:T(128)} %param.18) | copy-start | bytes 100
  37.4 183.1 %copy-start.6 = (s32[8]{0:T(128)S(1)}, s32[8]{0:T(128)}, u32[]{:S(2)}) copy-start(s32[8]{0:T(128)} %param.19) | copy-start | bytes 100
  37.4 183.9 %copy-start.1 = (f32[8,128]{1,0:T(8,128)S(1)}, f32[8,128]{1,0:T(8,128)}, u32[]{:S(2)}) copy-start(f32[8,128]{1,0:T(8,128)} %param.14) | copy-start | bytes 12292
  37.4 183.9 %copy-start.2 = (f32[8,128]{1,0:T(8,128)S(1)}, f32[8,128]{1,0:T(8,128)}, u32[]{:S(2)}) copy-start(f32[8,128]{1,0:T(8,128)} %param.15) | copy-start | bytes 12292
  37.5 183.9 %copy-start.3 = (f32[8,128]{1,0:T(8,128)S(1)}, f32[8,128]{1,0:T(8,128)}, u32[]{:S(2)}) copy-start(f32[8,128]{1,0:T(8,128)} %param.16) | copy-start | bytes 12292
  37.5 183.9 %copy-start.4 = (f32[8,128]{1,0:T(8,128)S(1)}, f32[8,128]{1,0:T(8,128)}, u32[]{:S(2)}) copy-start(f32[8,128]{1,0:T(8,128)} %param.17) | copy-start | bytes 12292
  213.6 251.6 %all-to-all-start = ((bf16[16,1536,256]{2,1,0:T(8,128)(2,1)}), bf16[16,1536,256]{2,1,0:T(8,128)(2,1)}, u32[]{:S(2)}, u32[]{:S(2)}) async-start(bf16[16,1536,256]{2,1,0:T(8,128)(2,1)} %gather_fusion), calls=%async_computation | async-start | bytes 25165824 | tf_op jit(solution)/shard_map/all_to_all | solution.py:93
  218.6 226.5 %all-reduce.6.cloned.1.call-start = ((), (), s32[]{:S(2)}) async-start(), calls=%async_computation.2 | async-start | bytes 655360 | tf_op jit(solution)/shard_map/psum | solution.py:101
  221.4 0.7 copy-start
  222.2 319.0 %all-reduce.8.cloned.1.call-start = ((), (), s32[]{:S(2)}) async-start(), calls=%async_computation.3 | async-start | bytes 3145728 | tf_op jit(solution)/shard_map/psum | solution.py:121
Sparse Core Ops, SparseCore 0:
  222.6 222.4 all-reduce.5
  477.8 63.3 all-reduce.7

commit v7 on v3

--- a/solution.py
+++ b/solution.py
@@ -1,3 +1,5 @@
+import functools
+
 import jax
 import jax.numpy as jnp
 from jax import lax
@@ -9,7 +11,7 @@
 K = 128
 S = 256
 WIN_DEV = 8
-NCH = 2
+NCH = 1
 TP = 1536
 
 
@@ -46,7 +48,7 @@
 
 def chunk_gram(source, snapshots, got, coef, chunk):
     nw, _, s = snapshots.shape
-    rows = got.shape[1]
+    rows = snapshots.shape[1] // NCH
     tp = min(TP, rows)
     nt = rows // tp
     base = chunk * nt
@@ -109,30 +111,36 @@
     hit = dest[None, :] == jnp.arange(nblocks, dtype=jnp.int32)[:, None]
     pick = jnp.sum(jnp.where(hit, jnp.arange(nw, dtype=jnp.int32)[None, :], 0), axis=1)
 
-    cp = rows // NCH
-    gots = []
-    for k in range(NCH):
-        sendbuf = send_buffer(pick, modes, k, cp)
-        gots.append(lax.all_to_all(sendbuf, "win", split_axis=0, concat_axis=0, tiled=True))
+    prm = jnp.stack([amp_re, amp_im, growth, freq], axis=1)
+    hi = lax.reduce_precision(prm, exponent_bits=8, mantissa_bits=7)
+    rest = prm - hi
+    mid = lax.reduce_precision(rest, exponent_bits=8, mantissa_bits=7)
+    low = rest - mid
+    parts = jnp.stack([hi, mid, low], axis=1).astype(jnp.bfloat16).reshape(nw, 6, s)
+    ints = jnp.zeros((nw, 2, s), jnp.float32)
+    ints = ints.at[:, 0, 0].set(mode_count.astype(jnp.float32))
+    ints = ints.at[:, 0, 1].set(slot_window.astype(jnp.float32))
+    prows = jnp.concatenate([parts, ints.astype(jnp.bfloat16)], axis=1)
+    payload = jnp.concatenate([modes, prows], axis=1)
+    sendbuf = jnp.take(payload, pick, axis=0, mode="clip")
+    got = lax.all_to_all(sendbuf, "win", split_axis=0, concat_axis=0, tiled=True)
+    gots = [got]
 
-    extra = jnp.zeros((nw, K), jnp.float32)
-    extra = extra.at[:, 0].set(mode_count.astype(jnp.float32))
-    extra = extra.at[:, 1].set(slot_window.astype(jnp.float32))
-    packed = jnp.concatenate([amp_re, amp_im, growth, freq, extra], axis=1)
-    packed_all = lax.all_gather(packed, "win", axis=0, tiled=True)
-    sw_all = packed_all[:, 4 * K + 1].astype(jnp.int32)
+    tail = got[:, rows:, :].astype(jnp.float32)
+    sw_got = tail[:, 6, 1].astype(jnp.int32)
     wins = me * WIN_DEV + jnp.arange(nw, dtype=jnp.int32)
-    slot_ids = jnp.arange(packed_all.shape[0], dtype=jnp.int32)
-    match = sw_all[None, :] == wins[:, None]
-    slot = jnp.sum(jnp.where(match, slot_ids[None, :], 0), axis=1)
-    source = slot // WIN_DEV
-    sel = jnp.sum(jnp.where(match[:, :, None], packed_all[None, :, :], 0.0), axis=1)
+    srcs = jnp.arange(nblocks, dtype=jnp.int32)
+    match = sw_got[None, :] == wins[:, None]
+    source = jnp.sum(jnp.where(match, srcs[None, :], 0), axis=1)
+    sel = jnp.sum(jnp.where(match[:, :, None, None], tail[None], 0.0), axis=1)
+    trip = sel[:, :6, :].reshape(nw, 3, 4, K)
+    prm_sel = (trip[:, 0] + trip[:, 1]) + trip[:, 2]
     coef = coefficients(
-        sel[:, 0:K],
-        sel[:, K : 2 * K],
-        sel[:, 2 * K : 3 * K],
-        sel[:, 3 * K : 4 * K],
-        sel[:, 4 * K].astype(jnp.int32),
+        prm_sel[:, 0],
+        prm_sel[:, 1],
+        prm_sel[:, 2],
+        prm_sel[:, 3],
+        sel[:, 6, 0].astype(jnp.int32),
     )
 
     part_sum = None

time: 530 us -> 567 us (1.070)
  waiting for transfers between devices: 236 us -> 438 us
  blocking collectives: 196 us -> 0 us
  local copies, waits for them, and re-layouts: 2.06 us -> 70.8 us
  Pallas kernels: 52.1 us -> 21.9 us
  starting transfers between devices: 14.2 us -> 8.35 us
    all_to_all x2 -> x1, waiting for transfers between devices: 172 us -> 377 us  [on_device(): lax.all_to_all(sendbuf, 'win', split_axis=0, concat_axis=0, tiled=True)]
    all_gather x1 -> x0, blocking collectives: 196 us -> none  [on_device(): packed_all = lax.all_gather(packed, 'win', axis=0, tiled=True)]
    concatenate x1, local copies, waits for them, and re-layouts: 0.01 us -> 52.2 us  [on_device(): payload = jnp.concatenate([modes, prows], axis=1)]
    pallas_call x2 -> x0, Pallas kernels: 29.8 us -> none  [send_buffer(): pl.pallas_call(copy_kernel, grid_spec=pltpu.PrefetchScalarGridSpec(num_sc...]
    gather x0 -> x1, local copies, waits for them, and re-layouts: none -> 14.5 us  [on_device(): sendbuf = jnp.take(payload, pick, axis=0, mode='clip')]
    all_to_all x2 -> x1, starting transfers between devices: 14.2 us -> 8.31 us  [on_device(): lax.all_to_all(sendbuf, 'win', split_axis=0, concat_axis=0, tiled=True)]
    pallas_call x2 -> x1, Pallas kernels: 22.3 us -> 21.9 us  [chunk_gram(): pl.pallas_call(gram_kernel, grid_spec=pltpu.PrefetchScalarGridSpec(num_sc...]
  transfers between devices with their start and end apart: 3 -> 2, of which waited for: 2 -> 2; matrix products, arithmetic and copies ran while one was open for 2% -> 0% of each run, Pallas kernels for 5% -> 0%
where the time goes in v7:
time: 567 us; the launch traced here: 565 us
  waiting for transfers between devices  438 us (77%)
  local copies, waits for them, and re-layouts  70.8 us (12%)
  Pallas kernels  21.9 us (4%)
  between operations  13.5 us (2%)
  other arithmetic  12 us (2%)
  starting transfers between devices  8.35 us (1%)
    all_to_all x1, waiting for transfers between devices, on_device(): lax.all_to_all(sendbuf, 'win', split_axis=0, concat_axis=0, tiled=True)  377 us
    psum x1, waiting for transfers between devices, on_device(): total = lax.psum(part_sum, 'space') / points_all  61.4 us
    concatenate x1, local copies, waits for them, and re-layouts, on_device(): payload = jnp.concatenate([modes, prows], axis=1)  52.2 us
    pallas_call x1, Pallas kernels, chunk_gram(): pl.pallas_call(gram_kernel, grid_spec=pltpu.PrefetchScalarGridSpec(num_sc...  21.9 us
    gather x1, local copies, waits for them, and re-layouts, on_device(): sendbuf = jnp.take(payload, pick, axis=0, mode='clip')  14.5 us
  transfers between devices with their start and end apart: 2, of which 2 were waited for; matrix products, arithmetic and copies ran while one was open for 0% of the time, Pallas kernels for 0%

profile of v7, /device:TPU:0, one launch (start us, length us, event | category | flops | bytes accessed | tf_op | source)
XLA Modules:
  0.0 564.9 jit_solution(12367865455841350123)
XLA Ops:
  6.5 0.7 reduce-precision_convert_fusion.1
  7.3 0.7 and_select_fusion
  8.0 0.1 copy.30
  8.1 0.6 fusion.17
  8.7 0.7 convert_bitcast_fusion.1
  9.4 0.1 copy.29
  9.5 1.4 scatter.9
  11.0 0.1 select_reduce_fusion.2
  11.1 52.2 %concatenate.38 = bf16[8,3080,256]{2,1,0:T(8,128)(2,1)} concatenate(bf16[8,3072,256]{2,1,0:T(8,128)(2,1)} %param.13, bf16[8,6,256]{2,1,0:T(8,128)(2,1)S(1)} %copy.31, bf16[8,2,256]{2,1,0:T(2,128)(2,1)S(1)} %copy.32), dimensions={1} | concatenate | bytes 25231360 | tf_op jit(solution)/shard_map/concatenate | solution.py:124
  63.2 14.5 %gather_fusion = bf16[16,3080,256]{2,1,0:T(8,128)(2,1)} fusion(bf16[8,3080,256]{2,1,0:T(8,128)(2,1)} %concatenate.38, s32[1024]{0:T(1024)S(1)} %pad_clamp_fusion), kind=kCustom, calls=%fused_computation | custom fusion | bytes 50462784 | tf_op jit(solution)/shard_map/jit(_take)/gather | solution.py:125
  77.7 8.3 %all-to-all-start = ((bf16[16,3080,256]{2,1,0:T(8,128)(2,1)}), bf16[16,3080,256]{2,1,0:T(8,128)(2,1)}, u32[]{:S(2)}, u32[]{:S(2)}) async-start(bf16[16,3080,256]{2,1,0:T(8,128)(2,1)} %gather_fusion), calls=%async_computation | async-start | bytes 50462720 | tf_op jit(solution)/shard_map/all_to_all | solution.py:126
  86.0 0.0 all-reduce.3.cloned.1.call-start
  86.1 376.9 %all-to-all-done.m_ref = bf16[16,3080,256]{2,1,0:T(8,128)(2,1)} async-done(((bf16[16,3080,256]{2,1,0:T(8,128)(2,1)}), bf16[16,3080,256]{2,1,0:T(8,128)(2,1)}, u32[]{:S(2)}, u32[]{:S(2)}) %all-to-all-start) | async-done | bytes 25231392 | tf_op jit(solution)/shard_map/all_to_all | solution.py:126
  463.0 0.8 slice_convert_fusion
  463.8 0.4 fusion.13
  464.3 0.1 broadcast_compare_fusion
  464.3 0.2 select_reduce_fusion.1.src_ref
  464.5 0.2 select_reduce_fusion
  464.7 0.2 fusion.14
  465.0 0.1 fusion.15
  465.1 4.5 fusion.6
  469.6 0.1 pad_maximum_fusion
  469.7 1.1 copy.34
  470.8 0.4 convert_element_type.67.c_ref
  471.3 21.9 %shard_map.82 = f32[8,128,384]{2,1,0:T(8,128)} custom-call(s32[8]{0:T(128)S(1)} %select_reduce_fusion.1.src_ref, bf16[8,3072,256]{2,1,0:T(8,128)(2,1)} %s_ref.1, bf16[16,3080,256]{2,1,0:T(8,128)(2,1)} %all-to-all-done.m_ref, bf16[8,256,256]{2,1,0:T(8,128)(2,1)S(1)} %convert_element_type.67.c_ref), custom_call_target="tpu_custom_call" | custom-call | flops 5637144576 | bytes 25165824 | tf_op jit(solution)/shard_map/pallas_call | solution.py:55
  493.2 0.0 all-reduce.3.cloned.1.call-update
  493.2 61.4 %all-reduce.3.cloned.1.call-done = f32[8,128,384]{2,1,0:T(8,128)} async-done(((f32[8,128,384]{2,1,0:T(8,128)}), f32[8,128,384]{2,1,0:T(8,128)}) %all-reduce.3.cloned.1.call-update) | async-done | bytes 1572880 | tf_op jit(solution)/shard_map/psum | solution.py:150
  554.6 1.5 broadcast_multiply_fusion
  556.2 0.1 fusion.16
  556.3 0.1 slice.116
  556.4 0.2 copy.36
  556.6 1.5 maximum_maximum_fusion
  (11 shorter events, 0.1 us)
Async XLA Ops:
  77.7 385.3 %all-to-all-start = ((bf16[16,3080,256]{2,1,0:T(8,128)(2,1)}), bf16[16,3080,256]{2,1,0:T(8,128)(2,1)}, u32[]{:S(2)}, u32[]{:S(2)}) async-start(bf16[16,3080,256]{2,1,0:T(8,128)(2,1)} %gather_fusion), calls=%async_computation | async-start | bytes 50462720 | tf_op jit(solution)/shard_map/all_to_all | solution.py:126
  86.0 468.6 %all-reduce.3.cloned.1.call-start = ((), (), s32[]{:S(2)}) async-start(), calls=%async_computation.1 | async-start | bytes 3145728 | tf_op jit(solution)/shard_map/psum | solution.py:150
Sparse Core Ops, SparseCore 0:
  493.3 61.2 all-reduce.2

commit v8 on v6

--- a/solution.py
+++ b/solution.py
@@ -96,9 +96,7 @@
     extra = extra.at[:, 0].set(mode_count.astype(jnp.float32))
     extra = extra.at[:, 1].set(slot_window.astype(jnp.float32))
     packed = jnp.concatenate([amp_re, amp_im, growth, freq, extra], axis=1)
-    spread = jnp.zeros((nblocks,) + packed.shape, jnp.float32)
-    spread = lax.dynamic_update_slice(spread, packed[None], (me, 0, 0))
-    packed_all = lax.psum(spread, "win").reshape((-1, packed.shape[1]))
+    packed_all = lax.all_gather(packed, "win", axis=0, tiled=True)
     sw_all = packed_all[:, 4 * K + 1].astype(jnp.int32)
     wins = me * WIN_DEV + jnp.arange(nw, dtype=jnp.int32)
     slot_ids = jnp.arange(packed_all.shape[0], dtype=jnp.int32)
@@ -118,7 +116,11 @@
     for k in range(NCH):
         g = chunk_gram(source, snapshots, gots[k], coef, k)
         part_sum = g if part_sum is None else part_sum + g
-    total = lax.psum(part_sum, "space") / points_all
+    nsp = lax.axis_size("space")
+    mine = lax.all_to_all(part_sum, "space", split_axis=0, concat_axis=0, tiled=True)
+    red = jnp.sum(mine.reshape((nsp, nw // nsp) + mine.shape[1:]), axis=0)
+    spread = jnp.broadcast_to(red[None], (nsp,) + red.shape).reshape((nsp * red.shape[0],) + red.shape[1:])
+    total = lax.all_to_all(spread, "space", split_axis=0, concat_axis=0, tiled=True) / points_all
     half = s // 2
     top = total[:, :, :s]
     mid = total[:, :, half:s]

time: 552 us -> 494 us (0.89)
  waiting for transfers between devices: 462 us -> 176 us
  blocking collectives: 0 us -> 246 us
  between operations: 13.7 us -> 0.24 us
    psum x2 -> x0, waiting for transfers between devices: 286 us -> none  [the longest x1 223 us: on_device(): packed_all = lax.psum(spread, 'win').reshape((-1, packed.shape[1]))]
    all_gather x0 -> x1, blocking collectives: none -> 196 us  [on_device(): packed_all = lax.all_gather(packed, 'win', axis=0, tiled=True)]
    all_to_all x0 -> x2, blocking collectives: none -> 49.7 us  [the longest x1 25.7 us: on_device(): lax.all_to_all(part_sum, 'space', split_axis=0, concat_axis=0, tiled=True)]
  transfers between devices with their start and end apart: 4 -> 2, of which waited for: 3 -> 1; matrix products, arithmetic and copies ran while one was open for 4% -> 4% of each run, Pallas kernels for 2% -> 2%
where the time goes in v8:
time: 494 us; the launch traced here: 493 us
  blocking collectives  246 us (50%)
  waiting for transfers between devices  176 us (36%)
  local copies, waits for them, and re-layouts  24.1 us (5%)
  Pallas kernels  22.3 us (5%)
  starting transfers between devices  13.2 us (3%)
  other arithmetic  10.8 us (2%)
    all_gather x1, blocking collectives, on_device(): packed_all = lax.all_gather(packed, 'win', axis=0, tiled=True)  196 us
    all_to_all x2, waiting for transfers between devices, on_device(): lax.all_to_all(sendbuf, 'win', split_axis=0, concat_axis=0, tiled=True)  176 us
    all_to_all x1, blocking collectives, on_device(): lax.all_to_all(part_sum, 'space', split_axis=0, concat_axis=0, tiled=True)  25.7 us
    all_to_all x1, blocking collectives, on_device(): lax.all_to_all(spread, 'space', split_axis=0, concat_axis=0, tiled=True)  24 us
    pallas_call x2, Pallas kernels, chunk_gram(): pl.pallas_call(gram_kernel, grid_spec=pltpu.PrefetchScalarGridSpec(num_sc...  22.3 us
    gather x2, local copies, waits for them, and re-layouts, on_device(): sendbuf = modes_r[pick, k]  21.9 us
    all_to_all x2, starting transfers between devices, on_device(): lax.all_to_all(sendbuf, 'win', split_axis=0, concat_axis=0, tiled=True)  13.2 us
  transfers between devices with their start and end apart: 2, of which 1 were waited for; matrix products, arithmetic and copies ran while one was open for 4% of the time, Pallas kernels for 2%

profile of v8, /device:TPU:0, one launch (start us, length us, event | category | flops | bytes accessed | tf_op | source)
XLA Modules:
  0.0 492.9 jit_solution(13343759486110504848)
XLA Ops:
  0.0 0.7 and_select_fusion
  0.7 0.1 select_reduce_fusion.1
  0.8 11.0 %gather_fusion.1 = bf16[16,1536,256]{2,1,0:T(8,128)(2,1)} fusion(bf16[8,2,1536,256]{3,2,1,0:T(8,128)(2,1)} %bitcast.17, s32[16]{0:T(128)S(1)} %get-tuple-element.37), kind=kCustom, calls=%fused_computation.1 | custom fusion | bytes 25165952 | tf_op jit(solution)/shard_map/gather | solution.py:92
  11.8 8.2 %all-to-all-start.1 = ((bf16[16,1536,256]{2,1,0:T(8,128)(2,1)}), bf16[16,1536,256]{2,1,0:T(8,128)(2,1)}, u32[]{:S(2)}, u32[]{:S(2)}) async-start(bf16[16,1536,256]{2,1,0:T(8,128)(2,1)} %gather_fusion.1), calls=%async_computation.1 | async-start | bytes 25165824 | tf_op jit(solution)/shard_map/all_to_all | solution.py:93
  20.0 10.9 %gather_fusion = bf16[16,1536,256]{2,1,0:T(8,128)(2,1)} fusion(bf16[8,2,1536,256]{3,2,1,0:T(8,128)(2,1)} %bitcast.18, s32[16]{0:T(128)S(1)} %get-tuple-element.38), kind=kCustom, calls=%fused_computation | custom fusion | bytes 25165952 | tf_op jit(solution)/shard_map/gather | solution.py:92
  30.9 0.0 copy-start.4
  30.9 0.0 copy-start.5
  30.9 0.0 copy-start
  30.9 0.0 copy-start.1
  30.9 0.0 copy-start.2
  30.9 0.0 copy-start.3
  30.9 176.1 %all-to-all-done.1.m_ref = bf16[16,1536,256]{2,1,0:T(8,128)(2,1)} async-done(((bf16[16,1536,256]{2,1,0:T(8,128)(2,1)}), bf16[16,1536,256]{2,1,0:T(8,128)(2,1)}, u32[]{:S(2)}, u32[]{:S(2)}) %all-to-all-start.1) | async-done | bytes 12582944 | tf_op jit(solution)/shard_map/all_to_all | solution.py:93
  207.0 5.0 %all-to-all-start = ((bf16[16,1536,256]{2,1,0:T(8,128)(2,1)}), bf16[16,1536,256]{2,1,0:T(8,128)(2,1)}, u32[]{:S(2)}, u32[]{:S(2)}) async-start(bf16[16,1536,256]{2,1,0:T(8,128)(2,1)} %gather_fusion), calls=%async_computation | async-start | bytes 25165824 | tf_op jit(solution)/shard_map/all_to_all | solution.py:93
  212.0 0.6 compare_reduce_fusion.1
  212.7 0.0 copy-done.4
  212.7 0.6 fusion.14
  213.3 0.6 compare_reduce_fusion
  214.0 0.0 copy-done.5
  214.0 0.6 fusion.15
  214.7 0.1 copy.35
  214.7 0.0 copy-done
  214.7 0.0 copy-done.1
  214.8 0.0 copy-done.2
  214.8 0.0 copy-done.3
  214.8 196.4 %all_gather.3 = f32[128,640]{1,0:T(8,128)S(1)} all-gather(f32[8,640]{1,0:T(8,128)S(1)} %constant_dynamic-update-slice_fusion), channel_id=1, replica_groups=mesh['space'=8,'win'=16] {'win'}, dimensions={0}, use_global_device_ids=true | all-gather | bytes 348160 | tf_op jit(solution)/shard_map/all_gather | solution.py:99
  411.3 0.2 fusion.11
  411.4 0.1 broadcast_compare_fusion
  411.5 0.3 select_reduce_fusion
  411.8 0.1 fusion.12
  411.9 0.1 fusion.13
  412.0 4.5 fusion.6
  416.5 0.1 pad_maximum_fusion
  416.7 1.1 copy.36
  417.7 0.4 convert_element_type.49.c_ref
  418.2 0.2 select_reduce_fusion.2
  418.4 11.2 %shard_map.83 = f32[8,128,384]{2,1,0:T(8,128)S(1)} custom-call(s32[8]{0:T(128)S(1)} %and_select_fusion.1.src_ref, bf16[8,3072,256]{2,1,0:T(8,128)(2,1)} %s_ref.3, bf16[16,1536,256]{2,1,0:T(8,128)(2,1)} %all-to-all-done.1.m_ref, bf16[8,256,256]{2,1,0:T(8,128)(2,1)S(1)} %convert_element_type.49.c_ref), custom_call_target="tpu_custom_call" | custom-call | flops 2818572288 | bytes 12582912 | tf_op jit(solution)/shard_map/pallas_call | solution.py:53
  429.6 0.0 all-to-all-done.m_ref
  429.6 11.2 %shard_map.82 = f32[8,128,384]{2,1,0:T(8,128)S(1)} custom-call(s32[8]{0:T(128)S(1)} %and_select_fusion.1.src_ref, bf16[8,3072,256]{2,1,0:T(8,128)(2,1)} %s_ref.3, bf16[16,1536,256]{2,1,0:T(8,128)(2,1)} %all-to-all-done.m_ref, bf16[8,256,256]{2,1,0:T(8,128)(2,1)S(1)} %convert_element_type.49.c_ref), custom_call_target="tpu_custom_call" | custom-call | flops 2818572288 | bytes 12582912 | tf_op jit(solution)/shard_map/pallas_call | solution.py:53
  440.7 0.2 add.50
  440.9 25.7 %all_to_all.20 = f32[8,128,384]{2,1,0:T(8,128)S(1)} all-to-all(f32[8,128,384]{2,1,0:T(8,128)S(1)} %add.50), channel_id=1, replica_groups=mesh['space'=8,'win'=16] {'space'}, dimensions={0} | all-to-all | bytes 3145728 | tf_op jit(solution)/shard_map/all_to_all | solution.py:120
  466.6 0.1 reduce_sum.42
  466.7 0.1 reshape.198
  466.8 24.0 %all_to_all.21 = f32[8,128,384]{2,1,0:T(8,128)S(1)} all-to-all(f32[8,128,384]{2,1,0:T(8,128)S(1)} %reshape.198), channel_id=1, replica_groups=mesh['space'=8,'win'=16] {'space'}, dimensions={0} | all-to-all | bytes 3145728 | tf_op jit(solution)/shard_map/all_to_all | solution.py:123
  490.8 0.1 broadcast_multiply_fusion
  491.0 0.1 slice.75
  491.1 0.1 slice_bitcast_fusion
  491.2 0.2 copy.37
  491.4 1.5 maximum_maximum_fusion
  (12 shorter events, 0.1 us)
Async XLA Ops:
  11.8 195.2 %all-to-all-start.1 = ((bf16[16,1536,256]{2,1,0:T(8,128)(2,1)}), bf16[16,1536,256]{2,1,0:T(8,128)(2,1)}, u32[]{:S(2)}, u32[]{:S(2)}) async-start(bf16[16,1536,256]{2,1,0:T(8,128)(2,1)} %gather_fusion.1), calls=%async_computation.1 | async-start | bytes 25165824 | tf_op jit(solution)/shard_map/all_to_all | solution.py:93
  30.9 181.8 %copy-start.4 = (s32[8]{0:T(128)S(1)}, s32[8]{0:T(128)}, u32[]{:S(2)}) copy-start(s32[8]{0:T(128)} %param.18) | copy-start | bytes 100
  30.9 183.1 %copy-start.5 = (s32[8]{0:T(128)S(1)}, s32[8]{0:T(128)}, u32[]{:S(2)}) copy-start(s32[8]{0:T(128)} %param.19) | copy-start | bytes 100
  30.9 183.8 %copy-start = (f32[8,128]{1,0:T(8,128)S(1)}, f32[8,128]{1,0:T(8,128)}, u32[]{:S(2)}) copy-start(f32[8,128]{1,0:T(8,128)} %param.14) | copy-start | bytes 12292
  30.9 183.8 %copy-start.1 = (f32[8,128]{1,0:T(8,128)S(1)}, f32[8,128]{1,0:T(8,128)}, u32[]{:S(2)}) copy-start(f32[8,128]{1,0:T(8,128)} %param.15) | copy-start | bytes 12292
  30.9 183.8 %copy-start.2 = (f32[8,128]{1,0:T(8,128)S(1)}, f32[8,128]{1,0:T(8,128)}, u32[]{:S(2)}) copy-start(f32[8,128]{1,0:T(8,128)} %param.16) | copy-start | bytes 12292
  30.9 183.9 %copy-start.3 = (f32[8,128]{1,0:T(8,128)S(1)}, f32[8,128]{1,0:T(8,128)}, u32[]{:S(2)}) copy-start(f32[8,128]{1,0:T(8,128)} %param.17) | copy-start | bytes 12292
  207.0 222.5 %all-to-all-start = ((bf16[16,1536,256]{2,1,0:T(8,128)(2,1)}), bf16[16,1536,256]{2,1,0:T(8,128)(2,1)}, u32[]{:S(2)}, u32[]{:S(2)}) async-start(bf16[16,1536,256]{2,1,0:T(8,128)(2,1)} %gather_fusion), calls=%async_computation | async-start | bytes 25165824 | tf_op jit(solution)/shard_map/all_to_all | solution.py:93

commit v9 on v8

--- a/solution.py
+++ b/solution.py
@@ -116,16 +116,32 @@
     for k in range(NCH):
         g = chunk_gram(source, snapshots, gots[k], coef, k)
         part_sum = g if part_sum is None else part_sum + g
+    half = s // 2
+    blk_a = part_sum[:, :, :half]
+    blk_b = part_sum[:, :, half:s]
+    blk_d = part_sum[:, :, s:]
+    ii = jnp.arange(half, dtype=jnp.int32)[:, None]
+    jj = jnp.arange(half, dtype=jnp.int32)[None, :]
+    upper = ii <= jj
+    merged = jnp.where(upper[None], blk_a, blk_d)
+    diag_d = jnp.sum(jnp.where((ii == jj)[None], blk_d, 0.0), axis=1)
+    extra_row = jnp.concatenate([diag_d, jnp.zeros_like(diag_d)], axis=1)[:, None, :]
+    packed_g = jnp.concatenate([jnp.concatenate([blk_b, merged], axis=2), extra_row], axis=1)
+
     nsp = lax.axis_size("space")
-    mine = lax.all_to_all(part_sum, "space", split_axis=0, concat_axis=0, tiled=True)
+    mine = lax.all_to_all(packed_g, "space", split_axis=0, concat_axis=0, tiled=True)
     red = jnp.sum(mine.reshape((nsp, nw // nsp) + mine.shape[1:]), axis=0)
     spread = jnp.broadcast_to(red[None], (nsp,) + red.shape).reshape((nsp * red.shape[0],) + red.shape[1:])
     total = lax.all_to_all(spread, "space", split_axis=0, concat_axis=0, tiled=True) / points_all
-    half = s // 2
-    top = total[:, :, :s]
-    mid = total[:, :, half:s]
-    low = total[:, :, s:]
-    bottom = jnp.concatenate([jnp.swapaxes(mid, 1, 2), low], axis=2)
+
+    tb = total[:, :half, :half]
+    tm = total[:, :half, half:]
+    tmt = jnp.swapaxes(tm, 1, 2)
+    tdiag = total[:, half, :half]
+    ta = jnp.where(upper[None], tm, tmt)
+    td = jnp.where((ii > jj)[None], tm, jnp.where((ii < jj)[None], tmt, tdiag[:, None, :]))
+    top = jnp.concatenate([ta, tb], axis=2)
+    bottom = jnp.concatenate([jnp.swapaxes(tb, 1, 2), td], axis=2)
     return jnp.concatenate([top, bottom], axis=1)
 
 

time: 494 us -> 494 us (level)
  blocking collectives: 246 us -> 217 us
  waiting for transfers between devices: 176 us -> 193 us
  local copies, waits for them, and re-layouts: 24.1 us -> 29.6 us
    all_to_all x2 -> x1, blocking collectives: 49.7 us -> 20.8 us  [on_device(): lax.all_to_all(packed_g, 'space', split_axis=0, concat_axis=0, tiled=True)]
    all_to_all x0 -> x1, waiting for transfers between devices: none -> 16.5 us  [on_device(): lax.all_to_all(spread, 'space', split_axis=0, concat_axis=0, tiled=True)]
  transfers between devices with their start and end apart: 2 -> 3, of which waited for: 1 -> 2; matrix products, arithmetic and copies ran while one was open for 4% -> 4% of each run, Pallas kernels for 2% -> 2%
where the time goes in v9:
time: 494 us; the launch traced here: 493 us
  blocking collectives  217 us (44%)
  waiting for transfers between devices  193 us (39%)
  local copies, waits for them, and re-layouts  29.6 us (6%)
  Pallas kernels  22.3 us (5%)
  starting transfers between devices  16.8 us (3%)
  other arithmetic  13.9 us (3%)
    all_gather x1, blocking collectives, on_device(): packed_all = lax.all_gather(packed, 'win', axis=0, tiled=True)  196 us
    all_to_all x2, waiting for transfers between devices, on_device(): lax.all_to_all(sendbuf, 'win', split_axis=0, concat_axis=0, tiled=True)  176 us
    pallas_call x2, Pallas kernels, chunk_gram(): pl.pallas_call(gram_kernel, grid_spec=pltpu.PrefetchScalarGridSpec(num_sc...  22.3 us
    gather x2, local copies, waits for them, and re-layouts, on_device(): sendbuf = modes_r[pick, k]  21.9 us
    all_to_all x1, blocking collectives, on_device(): lax.all_to_all(packed_g, 'space', split_axis=0, concat_axis=0, tiled=True)  20.8 us
    all_to_all x1, waiting for transfers between devices, on_device(): lax.all_to_all(spread, 'space', split_axis=0, concat_axis=0, tiled=True)  16.5 us
    all_to_all x2, starting transfers between devices, on_device(): lax.all_to_all(sendbuf, 'win', split_axis=0, concat_axis=0, tiled=True)  13.2 us
  transfers between devices with their start and end apart: 3, of which 2 were waited for; matrix products, arithmetic and copies ran while one was open for 4% of the time, Pallas kernels for 2%

profile of v9, /device:TPU:0, one launch (start us, length us, event | category | flops | bytes accessed | tf_op | source)
XLA Modules:
  0.0 492.7 jit_solution(4969494965921401270)
XLA Ops:
  0.0 0.7 and_select_fusion
  0.7 0.1 select_reduce_fusion.2
  0.8 11.0 %gather_fusion.1 = bf16[16,1536,256]{2,1,0:T(8,128)(2,1)} fusion(bf16[8,2,1536,256]{3,2,1,0:T(8,128)(2,1)} %bitcast.22, s32[16]{0:T(128)S(1)} %get-tuple-element.43), kind=kCustom, calls=%fused_computation.1 | custom fusion | bytes 25165952 | tf_op jit(solution)/shard_map/gather | solution.py:92
  11.8 8.2 %all-to-all-start.1 = ((bf16[16,1536,256]{2,1,0:T(8,128)(2,1)}), bf16[16,1536,256]{2,1,0:T(8,128)(2,1)}, u32[]{:S(2)}, u32[]{:S(2)}) async-start(bf16[16,1536,256]{2,1,0:T(8,128)(2,1)} %gather_fusion.1), calls=%async_computation.1 | async-start | bytes 25165824 | tf_op jit(solution)/shard_map/all_to_all | solution.py:93
  20.0 10.9 %gather_fusion = bf16[16,1536,256]{2,1,0:T(8,128)(2,1)} fusion(bf16[8,2,1536,256]{3,2,1,0:T(8,128)(2,1)} %bitcast.23, s32[16]{0:T(128)S(1)} %get-tuple-element.44), kind=kCustom, calls=%fused_computation | custom fusion | bytes 25165952 | tf_op jit(solution)/shard_map/gather | solution.py:92
  30.9 0.0 copy-start.6
  30.9 0.0 copy-start.7
  30.9 0.0 copy-start.2
  30.9 0.0 copy-start.3
  30.9 0.0 copy-start.4
  30.9 0.0 copy-start.5
  30.9 176.1 %all-to-all-done.1.m_ref = bf16[16,1536,256]{2,1,0:T(8,128)(2,1)} async-done(((bf16[16,1536,256]{2,1,0:T(8,128)(2,1)}), bf16[16,1536,256]{2,1,0:T(8,128)(2,1)}, u32[]{:S(2)}, u32[]{:S(2)}) %all-to-all-start.1) | async-done | bytes 12582944 | tf_op jit(solution)/shard_map/all_to_all | solution.py:93
  207.0 5.0 %all-to-all-start = ((bf16[16,1536,256]{2,1,0:T(8,128)(2,1)}), bf16[16,1536,256]{2,1,0:T(8,128)(2,1)}, u32[]{:S(2)}, u32[]{:S(2)}) async-start(bf16[16,1536,256]{2,1,0:T(8,128)(2,1)} %gather_fusion), calls=%async_computation | async-start | bytes 25165824 | tf_op jit(solution)/shard_map/all_to_all | solution.py:93
  212.0 0.6 compare_reduce_fusion.1
  212.7 0.0 copy-done.6
  212.7 0.6 fusion.15
  213.3 0.6 compare_reduce_fusion
  214.0 0.0 copy-done.7
  214.0 0.6 fusion.16
  214.7 0.1 copy.61
  214.7 0.0 copy-done.2
  214.7 0.0 copy-done.3
  214.8 0.0 copy-done.4
  214.8 0.0 copy-done.5
  214.8 196.4 %all_gather.3 = f32[128,640]{1,0:T(8,128)S(1)} all-gather(f32[8,640]{1,0:T(8,128)S(1)} %constant_dynamic-update-slice_fusion), channel_id=1, replica_groups=mesh['space'=8,'win'=16] {'win'}, dimensions={0}, use_global_device_ids=true | all-gather | bytes 348160 | tf_op jit(solution)/shard_map/all_gather | solution.py:99
  411.3 0.2 fusion.12
  411.4 0.1 broadcast_compare_fusion
  411.5 0.3 select_reduce_fusion
  411.8 0.1 fusion.13
  411.9 0.1 fusion.14
  412.0 4.5 fusion.6
  416.5 0.1 pad_maximum_fusion.1
  416.7 1.1 copy.62
  417.7 0.4 convert_element_type.49.c_ref
  418.2 0.2 select_reduce_fusion.3
  418.4 11.2 %shard_map.83 = f32[8,128,384]{2,1,0:T(8,128)S(1)} custom-call(s32[8]{0:T(128)S(1)} %and_select_fusion.1.src_ref, bf16[8,3072,256]{2,1,0:T(8,128)(2,1)} %s_ref.3, bf16[16,1536,256]{2,1,0:T(8,128)(2,1)} %all-to-all-done.1.m_ref, bf16[8,256,256]{2,1,0:T(8,128)(2,1)S(1)} %convert_element_type.49.c_ref), custom_call_target="tpu_custom_call" | custom-call | flops 2818572288 | bytes 12582912 | tf_op jit(solution)/shard_map/pallas_call | solution.py:53
  429.6 0.0 all-to-all-done.m_ref
  429.6 11.2 %shard_map.82 = f32[8,128,384]{2,1,0:T(8,128)S(1)} custom-call(s32[8]{0:T(128)S(1)} %and_select_fusion.1.src_ref, bf16[8,3072,256]{2,1,0:T(8,128)(2,1)} %s_ref.3, bf16[16,1536,256]{2,1,0:T(8,128)(2,1)} %all-to-all-done.m_ref, bf16[8,256,256]{2,1,0:T(8,128)(2,1)S(1)} %convert_element_type.49.c_ref), custom_call_target="tpu_custom_call" | custom-call | flops 2818572288 | bytes 12582912 | tf_op jit(solution)/shard_map/pallas_call | solution.py:53
  440.8 0.2 add.52
  440.9 0.1 fusion.21
  441.1 0.1 pad_maximum_fusion
  441.2 20.8 %all_to_all.20 = f32[8,129,256]{2,1,0:T(8,128)S(1)} all-to-all(f32[8,129,256]{2,1,0:T(8,128)S(1)} %pad_maximum_fusion), channel_id=1, replica_groups=mesh['space'=8,'win'=16] {'space'}, dimensions={0} | all-to-all | bytes 2113536 | tf_op jit(solution)/shard_map/all_to_all | solution.py:132
  462.0 0.1 reduce_sum.52
  462.1 1.1 reshape.246
  463.1 3.6 all-to-all-start.3
  466.7 16.5 %all-to-all-done.3 = f32[8,129,256]{2,1,0:T(8,128)S(1)} async-done(((f32[8,129,256]{2,1,0:T(8,128)}), f32[8,129,256]{2,1,0:T(8,128)S(1)}, u32[]{:S(2)}, u32[]{:S(2)}) %all-to-all-start.3) | async-done | bytes 1056800 | tf_op jit(solution)/shard_map/all_to_all | solution.py:135
  483.2 1.7 copy.63
  485.0 1.8 broadcast_multiply_fusion
  486.8 1.0 fusion.20
  487.8 0.2 slice_reduce_fusion
  488.0 1.0 copy.64
  489.0 0.0 copy-start
  489.0 1.0 copy.65
  490.0 0.0 copy-start.1
  490.0 1.2 bitcast_select_fusion.1
  491.2 0.0 copy-done
  491.2 0.0 copy-done.1
  491.2 1.5 maximum_maximum_fusion
  (16 shorter events, 0.2 us)
Async XLA Ops:
  11.8 195.2 %all-to-all-start.1 = ((bf16[16,1536,256]{2,1,0:T(8,128)(2,1)}), bf16[16,1536,256]{2,1,0:T(8,128)(2,1)}, u32[]{:S(2)}, u32[]{:S(2)}) async-start(bf16[16,1536,256]{2,1,0:T(8,128)(2,1)} %gather_fusion.1), calls=%async_computation.1 | async-start | bytes 25165824 | tf_op jit(solution)/shard_map/all_to_all | solution.py:93
  30.9 181.8 %copy-start.6 = (s32[8]{0:T(128)S(1)}, s32[8]{0:T(128)}, u32[]{:S(2)}) copy-start(s32[8]{0:T(128)} %param.18) | copy-start | bytes 100
  30.9 183.1 %copy-start.7 = (s32[8]{0:T(128)S(1)}, s32[8]{0:T(128)}, u32[]{:S(2)}) copy-start(s32[8]{0:T(128)} %param.19) | copy-start | bytes 100
  30.9 183.8 %copy-start.2 = (f32[8,128]{1,0:T(8,128)S(1)}, f32[8,128]{1,0:T(8,128)}, u32[]{:S(2)}) copy-start(f32[8,128]{1,0:T(8,128)} %param.14) | copy-start | bytes 12292
  30.9 183.8 %copy-start.3 = (f32[8,128]{1,0:T(8,128)S(1)}, f32[8,128]{1,0:T(8,128)}, u32[]{:S(2)}) copy-start(f32[8,128]{1,0:T(8,128)} %param.15) | copy-start | bytes 12292
  30.9 183.8 %copy-start.4 = (f32[8,128]{1,0:T(8,128)S(1)}, f32[8,128]{1,0:T(8,128)}, u32[]{:S(2)}) copy-start(f32[8,128]{1,0:T(8,128)} %param.16) | copy-start | bytes 12292
  30.9 183.9 %copy-start.5 = (f32[8,128]{1,0:T(8,128)S(1)}, f32[8,128]{1,0:T(8,128)}, u32[]{:S(2)}) copy-start(f32[8,128]{1,0:T(8,128)} %param.17) | copy-start | bytes 12292
  207.0 222.6 %all-to-all-start = ((bf16[16,1536,256]{2,1,0:T(8,128)(2,1)}), bf16[16,1536,256]{2,1,0:T(8,128)(2,1)}, u32[]{:S(2)}, u32[]{:S(2)}) async-start(bf16[16,1536,256]{2,1,0:T(8,128)(2,1)} %gather_fusion), calls=%async_computation | async-start | bytes 25165824 | tf_op jit(solution)/shard_map/all_to_all | solution.py:93
  463.1 20.1 %all-to-all-start.3 = ((f32[8,129,256]{2,1,0:T(8,128)}), f32[8,129,256]{2,1,0:T(8,128)S(1)}, u32[]{:S(2)}, u32[]{:S(2)}) async-start(f32[8,129,256]{2,1,0:T(8,128)} %reshape.246), calls=%async_computation.3 | async-start | bytes 2228224 | tf_op jit(solution)/shard_map/all_to_all | solution.py:135
  489.0 2.2 copy-start
  490.0 1.2 copy-start.1

commit v10 on v9

--- a/solution.py
+++ b/solution.py
@@ -10,7 +10,7 @@
 S = 256
 WIN_DEV = 8
 NCH = 2
-TP = 1536
+TP = 768
 
 
 def coefficients(amp_re, amp_im, growth, freq, mode_count):
@@ -130,9 +130,9 @@
 
     nsp = lax.axis_size("space")
     mine = lax.all_to_all(packed_g, "space", split_axis=0, concat_axis=0, tiled=True)
-    red = jnp.sum(mine.reshape((nsp, nw // nsp) + mine.shape[1:]), axis=0)
+    red = jnp.sum(mine.reshape((nsp, nw // nsp) + mine.shape[1:]), axis=0) / points_all
     spread = jnp.broadcast_to(red[None], (nsp,) + red.shape).reshape((nsp * red.shape[0],) + red.shape[1:])
-    total = lax.all_to_all(spread, "space", split_axis=0, concat_axis=0, tiled=True) / points_all
+    total = lax.all_to_all(spread, "space", split_axis=0, concat_axis=0, tiled=True)
 
     tb = total[:, :half, :half]
     tm = total[:, :half, half:]

time: 494 us -> 496 us (level)
  Pallas kernels: 22.3 us -> 31.8 us
    pallas_call x2, Pallas kernels: 22.3 us -> 31.8 us  [chunk_gram(): pl.pallas_call(gram_kernel, grid_spec=pltpu.PrefetchScalarGridSpec(num_sc...]
  transfers between devices with their start and end apart: 3 -> 3, of which waited for: 2 -> 2; matrix products, arithmetic and copies ran while one was open for 4% -> 4% of each run, Pallas kernels for 2% -> 3%
where the time goes in v10:
time: 496 us; the launch traced here: 495 us
  blocking collectives  217 us (44%)
  waiting for transfers between devices  193 us (39%)
  Pallas kernels  31.8 us (6%)
  local copies, waits for them, and re-layouts  25.1 us (5%)
  starting transfers between devices  16.8 us (3%)
  other arithmetic  11.1 us (2%)
    all_gather x1, blocking collectives, on_device(): packed_all = lax.all_gather(packed, 'win', axis=0, tiled=True)  196 us
    all_to_all x2, waiting for transfers between devices, on_device(): lax.all_to_all(sendbuf, 'win', split_axis=0, concat_axis=0, tiled=True)  176 us
    pallas_call x2, Pallas kernels, chunk_gram(): pl.pallas_call(gram_kernel, grid_spec=pltpu.PrefetchScalarGridSpec(num_sc...  31.8 us
    gather x2, local copies, waits for them, and re-layouts, on_device(): sendbuf = modes_r[pick, k]  21.9 us
    all_to_all x1, blocking collectives, on_device(): lax.all_to_all(packed_g, 'space', split_axis=0, concat_axis=0, tiled=True)  20.8 us
    all_to_all x1, waiting for transfers between devices, on_device(): lax.all_to_all(spread, 'space', split_axis=0, concat_axis=0, tiled=True)  16.5 us
    all_to_all x2, starting transfers between devices, on_device(): lax.all_to_all(sendbuf, 'win', split_axis=0, concat_axis=0, tiled=True)  13.2 us
  transfers between devices with their start and end apart: 3, of which 2 were waited for; matrix products, arithmetic and copies ran while one was open for 4% of the time, Pallas kernels for 3%

profile of v10, /device:TPU:0, one launch (start us, length us, event | category | flops | bytes accessed | tf_op | source)
XLA Modules:
  0.0 494.8 jit_solution(7272650369525346662)
XLA Ops:
  0.0 0.7 and_select_fusion
  0.7 0.1 select_reduce_fusion.2
  0.8 11.0 %gather_fusion.1 = bf16[16,1536,256]{2,1,0:T(8,128)(2,1)} fusion(bf16[8,2,1536,256]{3,2,1,0:T(8,128)(2,1)} %bitcast.24, s32[16]{0:T(128)S(1)} %get-tuple-element.41), kind=kCustom, calls=%fused_computation.1 | custom fusion | bytes 25165952 | tf_op jit(solution)/shard_map/gather | solution.py:92
  11.8 8.2 %all-to-all-start.1 = ((bf16[16,1536,256]{2,1,0:T(8,128)(2,1)}), bf16[16,1536,256]{2,1,0:T(8,128)(2,1)}, u32[]{:S(2)}, u32[]{:S(2)}) async-start(bf16[16,1536,256]{2,1,0:T(8,128)(2,1)} %gather_fusion.1), calls=%async_computation.1 | async-start | bytes 25165824 | tf_op jit(solution)/shard_map/all_to_all | solution.py:93
  20.0 10.9 %gather_fusion = bf16[16,1536,256]{2,1,0:T(8,128)(2,1)} fusion(bf16[8,2,1536,256]{3,2,1,0:T(8,128)(2,1)} %bitcast.25, s32[16]{0:T(128)S(1)} %get-tuple-element.42), kind=kCustom, calls=%fused_computation | custom fusion | bytes 25165952 | tf_op jit(solution)/shard_map/gather | solution.py:92
  30.9 0.0 copy-start.4
  30.9 0.0 copy-start.5
  30.9 0.0 copy-start
  30.9 0.0 copy-start.1
  30.9 0.0 copy-start.2
  30.9 0.0 copy-start.3
  30.9 176.1 %all-to-all-done.1.m_ref = bf16[16,1536,256]{2,1,0:T(8,128)(2,1)} async-done(((bf16[16,1536,256]{2,1,0:T(8,128)(2,1)}), bf16[16,1536,256]{2,1,0:T(8,128)(2,1)}, u32[]{:S(2)}, u32[]{:S(2)}) %all-to-all-start.1) | async-done | bytes 12582944 | tf_op jit(solution)/shard_map/all_to_all | solution.py:93
  207.0 5.0 %all-to-all-start = ((bf16[16,1536,256]{2,1,0:T(8,128)(2,1)}), bf16[16,1536,256]{2,1,0:T(8,128)(2,1)}, u32[]{:S(2)}, u32[]{:S(2)}) async-start(bf16[16,1536,256]{2,1,0:T(8,128)(2,1)} %gather_fusion), calls=%async_computation | async-start | bytes 25165824 | tf_op jit(solution)/shard_map/all_to_all | solution.py:93
  212.0 0.6 compare_reduce_fusion.1
  212.7 0.0 copy-done.4
  212.7 0.6 fusion.15
  213.3 0.6 compare_reduce_fusion
  214.0 0.0 copy-done.5
  214.0 0.6 fusion.16
  214.7 0.1 copy.69
  214.7 0.0 copy-done
  214.7 0.0 copy-done.1
  214.8 0.0 copy-done.2
  214.8 0.0 copy-done.3
  214.8 196.4 %all_gather.3 = f32[128,640]{1,0:T(8,128)S(1)} all-gather(f32[8,640]{1,0:T(8,128)S(1)} %constant_dynamic-update-slice_fusion), channel_id=1, replica_groups=mesh['space'=8,'win'=16] {'win'}, dimensions={0}, use_global_device_ids=true | all-gather | bytes 348160 | tf_op jit(solution)/shard_map/all_gather | solution.py:99
  411.3 0.2 fusion.12
  411.4 0.1 broadcast_compare_fusion
  411.5 0.3 select_reduce_fusion
  411.8 0.1 fusion.13
  411.9 0.1 fusion.14
  412.0 4.5 fusion.6
  416.5 0.1 pad_maximum_fusion.1
  416.7 1.1 copy.70
  417.7 0.4 convert_element_type.49.c_ref
  418.2 0.2 select_reduce_fusion.3
  418.4 15.9 %shard_map.83 = f32[8,128,384]{2,1,0:T(8,128)S(1)} custom-call(s32[8]{0:T(128)S(1)} %and_select_fusion.1.src_ref, bf16[8,3072,256]{2,1,0:T(8,128)(2,1)} %s_ref.3, bf16[16,1536,256]{2,1,0:T(8,128)(2,1)} %all-to-all-done.1.m_ref, bf16[8,256,256]{2,1,0:T(8,128)(2,1)S(1)} %convert_element_type.49.c_ref), custom_call_target="tpu_custom_call" | custom-call | flops 2818572288 | bytes 12582912 | tf_op jit(solution)/shard_map/pallas_call | solution.py:53
  434.3 0.0 all-to-all-done.m_ref
  434.3 15.9 %shard_map.82 = f32[8,128,384]{2,1,0:T(8,128)S(1)} custom-call(s32[8]{0:T(128)S(1)} %and_select_fusion.1.src_ref, bf16[8,3072,256]{2,1,0:T(8,128)(2,1)} %s_ref.3, bf16[16,1536,256]{2,1,0:T(8,128)(2,1)} %all-to-all-done.m_ref, bf16[8,256,256]{2,1,0:T(8,128)(2,1)S(1)} %convert_element_type.49.c_ref), custom_call_target="tpu_custom_call" | custom-call | flops 2818572288 | bytes 12582912 | tf_op jit(solution)/shard_map/pallas_call | solution.py:53
  450.2 0.2 add.52
  450.4 0.1 fusion.20
  450.5 0.1 pad_maximum_fusion
  450.6 20.8 %all_to_all.20 = f32[8,129,256]{2,1,0:T(8,128)S(1)} all-to-all(f32[8,129,256]{2,1,0:T(8,128)S(1)} %pad_maximum_fusion), channel_id=1, replica_groups=mesh['space'=8,'win'=16] {'space'}, dimensions={0} | all-to-all | bytes 2113536 | tf_op jit(solution)/shard_map/all_to_all | solution.py:132
  471.4 0.1 reduce_sum.52
  471.5 1.1 reshape.250
  472.6 3.6 all-to-all-start.3
  476.2 16.5 %all-to-all-done.3 = f32[8,129,256]{2,1,0:T(8,128)S(1)} async-done(((f32[8,129,256]{2,1,0:T(8,128)}), f32[8,129,256]{2,1,0:T(8,128)S(1)}, u32[]{:S(2)}, u32[]{:S(2)}) %all-to-all-start.3) | async-done | bytes 1056800 | tf_op jit(solution)/shard_map/all_to_all | solution.py:135
  492.7 0.2 copy.77
  493.0 0.2 bitcast_select_fusion.1
  493.2 0.2 copy.78
  493.4 1.5 maximum_maximum_fusion
  (19 shorter events, 0.2 us)
Async XLA Ops:
  11.8 195.2 %all-to-all-start.1 = ((bf16[16,1536,256]{2,1,0:T(8,128)(2,1)}), bf16[16,1536,256]{2,1,0:T(8,128)(2,1)}, u32[]{:S(2)}, u32[]{:S(2)}) async-start(bf16[16,1536,256]{2,1,0:T(8,128)(2,1)} %gather_fusion.1), calls=%async_computation.1 | async-start | bytes 25165824 | tf_op jit(solution)/shard_map/all_to_all | solution.py:93
  30.9 181.8 %copy-start.4 = (s32[8]{0:T(128)S(1)}, s32[8]{0:T(128)}, u32[]{:S(2)}) copy-start(s32[8]{0:T(128)} %param.18) | copy-start | bytes 100
  30.9 183.1 %copy-start.5 = (s32[8]{0:T(128)S(1)}, s32[8]{0:T(128)}, u32[]{:S(2)}) copy-start(s32[8]{0:T(128)} %param.19) | copy-start | bytes 100
  30.9 183.8 %copy-start = (f32[8,128]{1,0:T(8,128)S(1)}, f32[8,128]{1,0:T(8,128)}, u32[]{:S(2)}) copy-start(f32[8,128]{1,0:T(8,128)} %param.14) | copy-start | bytes 12292
  30.9 183.8 %copy-start.1 = (f32[8,128]{1,0:T(8,128)S(1)}, f32[8,128]{1,0:T(8,128)}, u32[]{:S(2)}) copy-start(f32[8,128]{1,0:T(8,128)} %param.15) | copy-start | bytes 12292
  30.9 183.8 %copy-start.2 = (f32[8,128]{1,0:T(8,128)S(1)}, f32[8,128]{1,0:T(8,128)}, u32[]{:S(2)}) copy-start(f32[8,128]{1,0:T(8,128)} %param.16) | copy-start | bytes 12292
  30.9 183.9 %copy-start.3 = (f32[8,128]{1,0:T(8,128)S(1)}, f32[8,128]{1,0:T(8,128)}, u32[]{:S(2)}) copy-start(f32[8,128]{1,0:T(8,128)} %param.17) | copy-start | bytes 12292
  207.0 227.3 %all-to-all-start = ((bf16[16,1536,256]{2,1,0:T(8,128)(2,1)}), bf16[16,1536,256]{2,1,0:T(8,128)(2,1)}, u32[]{:S(2)}, u32[]{:S(2)}) async-start(bf16[16,1536,256]{2,1,0:T(8,128)(2,1)} %gather_fusion), calls=%async_computation | async-start | bytes 25165824 | tf_op jit(solution)/shard_map/all_to_all | solution.py:93
  472.6 20.1 %all-to-all-start.3 = ((f32[8,129,256]{2,1,0:T(8,128)}), f32[8,129,256]{2,1,0:T(8,128)S(1)}, u32[]{:S(2)}, u32[]{:S(2)}) async-start(f32[8,129,256]{2,1,0:T(8,128)} %reshape.250), calls=%async_computation.3 | async-start | bytes 2228224 | tf_op jit(solution)/shard_map/all_to_all | solution.py:135

commit v11 on v10

--- a/solution.py
+++ b/solution.py
@@ -10,7 +10,7 @@
 S = 256
 WIN_DEV = 8
 NCH = 2
-TP = 768
+TP = 3072
 
 
 def coefficients(amp_re, amp_im, growth, freq, mode_count):
@@ -46,7 +46,7 @@
 
 def chunk_gram(source, snapshots, got, coef, chunk):
     nw, _, s = snapshots.shape
-    rows = got.shape[1]
+    rows = snapshots.shape[1] // NCH
     tp = min(TP, rows)
     nt = rows // tp
     base = chunk * nt
@@ -85,31 +85,41 @@
     hit = dest[None, :] == jnp.arange(nblocks, dtype=jnp.int32)[:, None]
     pick = jnp.sum(jnp.where(hit, jnp.arange(nw, dtype=jnp.int32)[None, :], 0), axis=1)
 
+    prm = jnp.stack([amp_re, amp_im, growth, freq], axis=1)
+    hi = lax.reduce_precision(prm, exponent_bits=8, mantissa_bits=7)
+    rest = prm - hi
+    mid = lax.reduce_precision(rest, exponent_bits=8, mantissa_bits=7)
+    low = rest - mid
+    parts = jnp.stack([hi, mid, low], axis=1).astype(jnp.bfloat16).reshape(nw, 6, s)
+    ints = jnp.zeros((nw, 2, s), jnp.float32)
+    ints = ints.at[:, 0, 0].set(mode_count.astype(jnp.float32))
+    ints = ints.at[:, 0, 1].set(slot_window.astype(jnp.float32))
+    prows = jnp.concatenate([parts, ints.astype(jnp.bfloat16)], axis=1)
+
     cp = rows // NCH
     modes_r = modes.reshape(nw, NCH, cp, s)
     gots = []
     for k in range(NCH):
         sendbuf = modes_r[pick, k]
+        if k == 0:
+            sendbuf = jnp.concatenate([sendbuf, jnp.take(prows, pick, axis=0, mode="clip")], axis=1)
         gots.append(lax.all_to_all(sendbuf, "win", split_axis=0, concat_axis=0, tiled=True))
 
-    extra = jnp.zeros((nw, K), jnp.float32)
-    extra = extra.at[:, 0].set(mode_count.astype(jnp.float32))
-    extra = extra.at[:, 1].set(slot_window.astype(jnp.float32))
-    packed = jnp.concatenate([amp_re, amp_im, growth, freq, extra], axis=1)
-    packed_all = lax.all_gather(packed, "win", axis=0, tiled=True)
-    sw_all = packed_all[:, 4 * K + 1].astype(jnp.int32)
+    tail = gots[0][:, cp:, :].astype(jnp.float32)
+    sw_got = tail[:, 6, 1].astype(jnp.int32)
     wins = me * WIN_DEV + jnp.arange(nw, dtype=jnp.int32)
-    slot_ids = jnp.arange(packed_all.shape[0], dtype=jnp.int32)
-    match = sw_all[None, :] == wins[:, None]
-    slot = jnp.sum(jnp.where(match, slot_ids[None, :], 0), axis=1)
-    source = slot // WIN_DEV
-    sel = jnp.sum(jnp.where(match[:, :, None], packed_all[None, :, :], 0.0), axis=1)
+    srcs = jnp.arange(nblocks, dtype=jnp.int32)
+    match = sw_got[None, :] == wins[:, None]
+    source = jnp.sum(jnp.where(match, srcs[None, :], 0), axis=1)
+    sel = jnp.sum(jnp.where(match[:, :, None, None], tail[None], 0.0), axis=1)
+    trip = sel[:, :6, :].reshape(nw, 3, 4, K)
+    prm_sel = (trip[:, 0] + trip[:, 1]) + trip[:, 2]
     coef = coefficients(
-        sel[:, 0:K],
-        sel[:, K : 2 * K],
-        sel[:, 2 * K : 3 * K],
-        sel[:, 3 * K : 4 * K],
-        sel[:, 4 * K].astype(jnp.int32),
+        prm_sel[:, 0],
+        prm_sel[:, 1],
+        prm_sel[:, 2],
+        prm_sel[:, 3],
+        sel[:, 6, 0].astype(jnp.int32),
     )
 
     part_sum = None

time: 496 us -> 470 us (0.948)
  blocking collectives: 217 us -> 20.8 us
  waiting for transfers between devices: 193 us -> 357 us
  other arithmetic: 11.1 us -> 22.8 us
  Pallas kernels: 31.8 us -> 22.3 us
    all_gather x1 -> x0, blocking collectives: 196 us -> none  [on_device(): packed_all = lax.all_gather(packed, 'win', axis=0, tiled=True)]
    all_to_all x2, waiting for transfers between devices: 176 us -> 341 us  [on_device(): lax.all_to_all(sendbuf, 'win', split_axis=0, concat_axis=0, tiled=True)]
    concatenate x0 -> x2, other arithmetic: none -> 11.6 us  [the longest x1 11.6 us: on_device(): jnp.concatenate([sendbuf, jnp.take(prows, pick, axis=0, mode='clip')], ax...]
    pallas_call x2, Pallas kernels: 31.8 us -> 22.3 us  [chunk_gram(): pl.pallas_call(gram_kernel, grid_spec=pltpu.PrefetchScalarGridSpec(num_sc...]
  transfers between devices with their start and end apart: 3 -> 3, of which waited for: 2 -> 3; matrix products, arithmetic and copies ran while one was open for 4% -> 4% of each run, Pallas kernels for 3% -> 2%
where the time goes in v11:
time: 470 us; the launch traced here: 469 us
  waiting for transfers between devices  357 us (76%)
  local copies, waits for them, and re-layouts  28.4 us (6%)
  other arithmetic  22.8 us (5%)
  Pallas kernels  22.3 us (5%)
  blocking collectives  20.8 us (4%)
  starting transfers between devices  16.7 us (4%)
    all_to_all x2, waiting for transfers between devices, on_device(): lax.all_to_all(sendbuf, 'win', split_axis=0, concat_axis=0, tiled=True)  341 us
    pallas_call x2, Pallas kernels, chunk_gram(): pl.pallas_call(gram_kernel, grid_spec=pltpu.PrefetchScalarGridSpec(num_sc...  22.3 us
    gather x2, local copies, waits for them, and re-layouts, on_device(): sendbuf = modes_r[pick, k]  22 us
    all_to_all x1, blocking collectives, on_device(): lax.all_to_all(packed_g, 'space', split_axis=0, concat_axis=0, tiled=True)  20.8 us
    all_to_all x1, waiting for transfers between devices, on_device(): lax.all_to_all(spread, 'space', split_axis=0, concat_axis=0, tiled=True)  16.5 us
    all_to_all x2, starting transfers between devices, on_device(): lax.all_to_all(sendbuf, 'win', split_axis=0, concat_axis=0, tiled=True)  13.2 us
    concatenate x1, other arithmetic, on_device(): jnp.concatenate([sendbuf, jnp.take(prows, pick, axis=0, mode='clip')], ax...  11.6 us
  transfers between devices with their start and end apart: 3, of which 3 were waited for; matrix products, arithmetic and copies ran while one was open for 4% of the time, Pallas kernels for 2%

profile of v11, /device:TPU:0, one launch (start us, length us, event | category | flops | bytes accessed | tf_op | source)
XLA Modules:
  0.0 468.6 jit_solution(13714915584898353504)
XLA Ops:
  0.0 0.7 and_select_fusion
  0.7 0.1 select_reduce_fusion.3
  0.8 0.7 convert_bitcast_fusion.1
  1.5 0.1 copy.68
  1.6 0.1 copy.69
  1.7 0.6 fusion.21
  2.3 0.7 reduce-precision_convert_fusion.1
  3.1 2.0 scatter.9
  5.1 0.6 gather_fusion.1
  5.7 11.0 %gather_fusion = bf16[16,1536,256]{2,1,0:T(8,128)(2,1)} fusion(bf16[8,2,1536,256]{3,2,1,0:T(8,128)(2,1)} %bitcast.43, s32[16]{0:T(128)S(1)} %get-tuple-element.45), kind=kCustom, calls=%fused_computation | custom fusion | bytes 25165952 | tf_op jit(solution)/shard_map/gather | solution.py:103
  16.7 11.6 %pad_maximum_fusion = bf16[16,1544,256]{2,1,0:T(8,128)(2,1)} fusion(bf16[16,8,256]{2,1,0:T(8,128)(2,1)S(1)} %gather_fusion.1, bf16[16,1536,256]{2,1,0:T(8,128)(2,1)} %gather_fusion), kind=kLoop, calls=%fused_computation.3 | loop fusion | flops 25296896 | bytes 25296896 | tf_op jit(solution)/shard_map/concatenate | solution.py:105
  28.3 8.2 %all-to-all-start = ((bf16[16,1544,256]{2,1,0:T(8,128)(2,1)}), bf16[16,1544,256]{2,1,0:T(8,128)(2,1)}, u32[]{:S(2)}, u32[]{:S(2)}) async-start(bf16[16,1544,256]{2,1,0:T(8,128)(2,1)} %pad_maximum_fusion), calls=%async_computation | async-start | bytes 25296896 | tf_op jit(solution)/shard_map/all_to_all | solution.py:106
  36.5 11.0 %gather_fusion.2 = bf16[16,1536,256]{2,1,0:T(8,128)(2,1)} fusion(bf16[8,2,1536,256]{3,2,1,0:T(8,128)(2,1)} %bitcast.44, s32[16]{0:T(128)S(1)} %get-tuple-element.44), kind=kCustom, calls=%fused_computation.2 | custom fusion | bytes 25165952 | tf_op jit(solution)/shard_map/gather | solution.py:103
  47.5 177.0 %all-to-all-done.m_ref = bf16[16,1544,256]{2,1,0:T(8,128)(2,1)} async-done(((bf16[16,1544,256]{2,1,0:T(8,128)(2,1)}), bf16[16,1544,256]{2,1,0:T(8,128)(2,1)}, u32[]{:S(2)}, u32[]{:S(2)}) %all-to-all-start) | async-done | bytes 12648480 | tf_op jit(solution)/shard_map/all_to_all | solution.py:106
  224.5 5.0 %all-to-all-start.1 = ((bf16[16,1536,256]{2,1,0:T(8,128)(2,1)}), bf16[16,1536,256]{2,1,0:T(8,128)(2,1)}, u32[]{:S(2)}, u32[]{:S(2)}) async-start(bf16[16,1536,256]{2,1,0:T(8,128)(2,1)} %gather_fusion.2), calls=%async_computation.1 | async-start | bytes 25165824 | tf_op jit(solution)/shard_map/all_to_all | solution.py:106
  229.6 0.9 slice_convert_fusion
  230.4 0.4 fusion.14
  230.9 0.1 broadcast_compare_fusion
  230.9 0.2 select_reduce_fusion
  231.2 0.2 fusion.15
  231.4 0.1 fusion.16
  231.5 4.5 fusion.6
  236.1 0.1 pad_maximum_fusion.2
  236.2 1.1 copy.72
  237.2 0.4 convert_element_type.67.c_ref
  237.7 0.2 select_reduce_fusion.2.src_ref
  237.9 11.2 %shard_map.82 = f32[8,128,384]{2,1,0:T(8,128)S(1)} custom-call(s32[8]{0:T(128)S(1)} %select_reduce_fusion.2.src_ref, bf16[8,3072,256]{2,1,0:T(8,128)(2,1)} %s_ref.3, bf16[16,1544,256]{2,1,0:T(8,128)(2,1)} %all-to-all-done.m_ref, bf16[8,256,256]{2,1,0:T(8,128)(2,1)S(1)} %convert_element_type.67.c_ref), custom_call_target="tpu_custom_call" | custom-call | flops 2818572288 | bytes 12582912 | tf_op jit(solution)/shard_map/pallas_call | solution.py:53
  249.1 163.8 %all-to-all-done.1.m_ref = bf16[16,1536,256]{2,1,0:T(8,128)(2,1)} async-done(((bf16[16,1536,256]{2,1,0:T(8,128)(2,1)}), bf16[16,1536,256]{2,1,0:T(8,128)(2,1)}, u32[]{:S(2)}, u32[]{:S(2)}) %all-to-all-start.1) | async-done | bytes 12582944 | tf_op jit(solution)/shard_map/all_to_all | solution.py:106
  412.9 11.2 %shard_map.83 = f32[8,128,384]{2,1,0:T(8,128)S(1)} custom-call(s32[8]{0:T(128)S(1)} %select_reduce_fusion.2.src_ref, bf16[8,3072,256]{2,1,0:T(8,128)(2,1)} %s_ref.3, bf16[16,1536,256]{2,1,0:T(8,128)(2,1)} %all-to-all-done.1.m_ref, bf16[8,256,256]{2,1,0:T(8,128)(2,1)S(1)} %convert_element_type.67.c_ref), custom_call_target="tpu_custom_call" | custom-call | flops 2818572288 | bytes 12582912 | tf_op jit(solution)/shard_map/pallas_call | solution.py:53
  424.0 0.2 add.64
  424.2 0.1 fusion.20
  424.4 0.1 pad_maximum_fusion.1
  424.5 20.8 %all_to_all.20 = f32[8,129,256]{2,1,0:T(8,128)S(1)} all-to-all(f32[8,129,256]{2,1,0:T(8,128)S(1)} %pad_maximum_fusion.1), channel_id=1, replica_groups=mesh['space'=8,'win'=16] {'space'}, dimensions={0} | all-to-all | bytes 2113536 | tf_op jit(solution)/shard_map/all_to_all | solution.py:142
  445.2 0.1 reduce_sum.52
  445.3 1.1 reshape.481
  446.4 3.6 all-to-all-start.3
  450.0 16.5 %all-to-all-done.3 = f32[8,129,256]{2,1,0:T(8,128)S(1)} async-done(((f32[8,129,256]{2,1,0:T(8,128)}), f32[8,129,256]{2,1,0:T(8,128)S(1)}, u32[]{:S(2)}, u32[]{:S(2)}) %all-to-all-start.3) | async-done | bytes 1056800 | tf_op jit(solution)/shard_map/all_to_all | solution.py:145
  466.6 0.2 copy.79
  466.8 0.2 bitcast_select_fusion.1
  467.0 0.2 copy.80
  467.2 1.5 maximum_maximum_fusion
  (19 shorter events, 0.2 us)
Async XLA Ops:
  28.3 196.2 %all-to-all-start = ((bf16[16,1544,256]{2,1,0:T(8,128)(2,1)}), bf16[16,1544,256]{2,1,0:T(8,128)(2,1)}, u32[]{:S(2)}, u32[]{:S(2)}) async-start(bf16[16,1544,256]{2,1,0:T(8,128)(2,1)} %pad_maximum_fusion), calls=%async_computation | async-start | bytes 25296896 | tf_op jit(solution)/shard_map/all_to_all | solution.py:106
  224.5 188.3 %all-to-all-start.1 = ((bf16[16,1536,256]{2,1,0:T(8,128)(2,1)}), bf16[16,1536,256]{2,1,0:T(8,128)(2,1)}, u32[]{:S(2)}, u32[]{:S(2)}) async-start(bf16[16,1536,256]{2,1,0:T(8,128)(2,1)} %gather_fusion.2), calls=%async_computation.1 | async-start | bytes 25165824 | tf_op jit(solution)/shard_map/all_to_all | solution.py:106
  446.4 20.1 %all-to-all-start.3 = ((f32[8,129,256]{2,1,0:T(8,128)}), f32[8,129,256]{2,1,0:T(8,128)S(1)}, u32[]{:S(2)}, u32[]{:S(2)}) async-start(f32[8,129,256]{2,1,0:T(8,128)} %reshape.481), calls=%async_computation.3 | async-start | bytes 2228224 | tf_op jit(solution)/shard_map/all_to_all | solution.py:145
